TPU v7x, 32 devices: a whole 2x2x4 slice. The times are simulated.
32 devices in a mesh: groups: 2 (over y), tm: 4 (over z), rec: 2 (over x), mp: 2 (over core).
Axes of the slice: x: 2, y: 2, z: 4, core: 2. Of those that a mesh axis runs over, the one named last changes fastest.
Arguments:
- frames: bfloat16 [8, 4096, 512], P(('groups', 'rec'), 'tm'), parts along dimension 0, may hold values from -6 to 6
- lengths: int32 [8], P(('groups', 'rec')), parts along dimension 0, may hold values from 1024 to 4096
- memory_in: bfloat16 [8, 64, 512], P(('groups', 'rec'), 'tm'), parts along dimension 0, may hold values from -6 to 6
- gain_attn: float32 [512], replicated, may hold values from 0.25 to 1.75
- w_query: bfloat16 [512, 512], P(None, 'mp')
- w_key: bfloat16 [512, 512], P(None, 'mp')
- w_value: bfloat16 [512, 512], P(None, 'mp'), may hold values from -0.25 to 0.25
- w_out: bfloat16 [512, 512], P('mp'), may hold values from -0.25 to 0.25
- gain_conv: float32 [512], replicated, may hold values from 0.25 to 1.75
- w_conv_in: bfloat16 [2, 512, 512], P(None, None, 'mp'), may hold values from -0.25 to 0.25
- w_depth: bfloat16 [31, 512], P(None, 'mp'), may hold values from -1 to 1
- w_conv_out: bfloat16 [512, 512], P('mp'), may hold values from -0.25 to 0.25
- gain_ffn: float32 [512], replicated, may hold values from 0.25 to 1.75
- w_ffn_in: bfloat16 [512, 2048], P(None, 'mp'), may hold values from -0.25 to 0.25
- w_ffn_out: bfloat16 [512, 2048], P(None, 'mp'), may hold values from -0.125 to 0.125
Outputs:
- output: bfloat16 [8, 4096, 512], P(('groups', 'rec'), ('tm', 'mp')), parts along dimension 0
- memory_out: bfloat16 [8, 64, 512], P(('groups', 'rec'), 'tm'), parts along dimension 0
There are 2 independent parts, one for each index of `groups`. A program takes and returns all parts, laid end to end along the dimension named above; an argument that names none is the same for every part. Nothing has to cross between parts.
Inputs may be any that keep to these rules, and one draw needn't show every extreme that they name: `lengths`: the number of valid frames of each recording; its frames from that index on are padding.
All inputs are finite; a program needn't handle non-finite values.
Results may differ from a plain program's by a relative error of at most 0.023.
Values may be sent and summed in bfloat16 or wider, within the bound.
No kernel may reach another device: no remote copies, remote signals or barrier semaphores. Data moves between devices by JAX's collectives and lax.ppermute only.
A program may use at most 128 MiB of HBM per device.

v0:
```python
import functools

import jax
import jax.numpy as jnp
from jax import lax
from jax.experimental import pallas as pl
from jax.experimental.pallas import tpu as pltpu
from jax.sharding import PartitionSpec as P


CK = 31
SEG = 64
LEFT = 32
LOOK = 16
DH = 64
EPSILON = 1e-05
NEGATIVE_FILL = -1e30

HALO = LEFT + SEG
CONV = 32
WINDOW = 2 * SEG + LEFT + LOOK

BF16 = jnp.bfloat16
F32 = jnp.float32


def norm_rows(rows, gain):
    average = jnp.mean(rows, axis=-1, keepdims=True)
    centred = rows - average
    spread = jnp.mean(centred * centred, axis=-1, keepdims=True)
    return centred * lax.rsqrt(spread + EPSILON) * gain


def dot(a, b):
    return jnp.dot(a, b, preferred_element_type=F32)


def dot_nt(a, b):
    return lax.dot_general(a, b, (((1,), (1,)), ((), ())), preferred_element_type=F32)


def gated(half_value, half_gate):
    return half_value + half_value * jnp.tanh(half_gate)


def load_around(rec, frames, halo, target, core, own, before, after, sems):
    def edges(side):
        if side == 0:
            pieces = [(halo, HALO - before, 0, before), (frames, own, before + own, after)]
        else:
            pieces = [(frames, own - before, 0, before), (halo, 0, before + own, after)]
        return [
            pltpu.make_async_copy(
                source.at[rec, pl.ds(at, size)], target.at[rec, pl.ds(to, size)], sems.at[1 + place]
            )
            for place, (source, at, to, size) in enumerate(pieces)
            if size
        ]

    body = pltpu.make_async_copy(
        frames.at[rec, pl.ds(pl.multiple_of(core * own, own), own)],
        target.at[rec, pl.ds(before, own)],
        sems.at[0],
    )

    def start():
        body.start()
        for side in range(2):

            @pl.when(core == side)
            def _():
                for copy in edges(side):
                    copy.start()

    def wait():
        body.wait()
        for side in range(2):

            @pl.when(core == side)
            def _():
                for copy in edges(side):
                    copy.wait()

    return start, wait


def attention_kernel(*refs, seg_block, blocks):
    lengths, frames, halo = refs[0:3]
    memory = refs[3 : 3 + blocks]
    weights = refs[3 + blocks : 11 + blocks]
    gain_attn = refs[11 + blocks]
    ctx_out, memory_out = refs[12 + blocks : 14 + blocks]
    (
        x_s,
        n_s,
        q_s,
        k_s,
        v_s,
        m_s,
        kb_s,
        vb_s,
        sq_s,
        ctx_s,
        sctx_s,
        bias_s,
        kcat_s,
        vcat_s,
        w_s,
        wa_s,
        sems,
        m_sems,
        w_sems,
        o_sems,
    ) = refs[14 + blocks :]
    rec_count, ext, width = x_s.shape
    own = ext - HALO - LOOK
    frame_count = frames.shape[1]
    bank = seg_block * blocks
    keys = kcat_s.shape[1]
    half = width // 2
    block = lax.axis_index("tm")
    core = lax.axis_index("mp")
    start = block * frame_count + core * own
    pairs = own // (2 * SEG)
    group_rows = 2 * SEG

    loads = [
        load_around(rec, frames, halo, x_s, core, own, HALO, LOOK, sems.at[rec])
        for rec in range(rec_count)
    ]
    loads[0][0]()
    memory_copies = [
        pltpu.make_async_copy(
            memory[at], m_s.at[:, pl.ds(at * seg_block, seg_block)], m_sems.at[at]
        )
        for at in range(blocks)
    ]
    targets = [w_s.at[at] for at in range(6)] + [wa_s.at[0], wa_s.at[1]]
    copies = [
        pltpu.make_async_copy(source, target, w_sems.at[at])
        for at, (source, target) in enumerate(zip(weights, targets))
    ]
    weight_copies, out_copies = copies[0:6], copies[6:8]
    for copy in weight_copies:
        copy.start()
    for load in loads[1:]:
        load[0]()
    for copy in memory_copies + out_copies:
        copy.start()
    kcat_s[...] = jnp.zeros_like(kcat_s)
    vcat_s[:, :, :, 0:128] = jnp.zeros(vcat_s.shape[0:3] + (128,), BF16)
    vcat_s[:, :, :, 128:256] = jnp.ones(vcat_s.shape[0:3] + (128,), BF16)
    wq_o, wq_p, wk_o, wk_p, wv_o, wv_p = [w_s.at[at] for at in range(6)]
    chunks = 3
    step = ext // chunks
    for rec in range(rec_count):
        loads[rec][1]()
        if rec == 0:
            for copy in weight_copies:
                copy.wait()
        for part in range(chunks):
            rows = pl.ds(part * step, step)
            normed = norm_rows(x_s[rec, rows, :].astype(F32), gain_attn[...]).astype(BF16)
            n_s[rec, rows, :] = normed
            for side, (wq, wk, wv) in enumerate(((wq_o, wk_o, wv_o), (wq_p, wk_p, wv_p))):
                cols = pl.ds(side * half, half)
                q_s[rec, rows, cols] = (dot(normed, wq[...]) * DH**-0.5).astype(BF16)
                k_s[rec, rows, cols] = dot(normed, wk[...]).astype(BF16)
                v_s[rec, rows, cols] = dot(normed, wv[...]).astype(BF16)

    mean_rows = pairs * 16
    row_id = lax.broadcasted_iota(jnp.int32, (mean_rows, own), 0)
    col_id = lax.broadcasted_iota(jnp.int32, (mean_rows, own), 1)
    seg_of_row = jnp.where((row_id & 15) < 2, (row_id >> 4) * 2 + (row_id & 15), -1)
    averaging = jnp.where(seg_of_row == (col_id >> 6), 1.0 / SEG, 0.0).astype(BF16)
    summary = jnp.concatenate(
        [dot(averaging, n_s[rec, HALO : HALO + own, :]).astype(BF16) for rec in range(rec_count)],
        axis=0,
    )
    for copy in memory_copies:
        copy.wait()
    bank_rows = m_s[...].reshape(rec_count * bank, width)
    for part, (wq, wk, wv) in enumerate(((wq_o, wk_o, wv_o), (wq_p, wk_p, wv_p))):
        cols = pl.ds(part * half, half)
        kb_s[:, :, cols] = dot(bank_rows, wk[...]).astype(BF16).reshape(rec_count, bank, half)
        vb_s[:, :, cols] = dot(bank_rows, wv[...]).astype(BF16).reshape(rec_count, bank, half)
        sq_s[:, cols] = (dot(summary, wq[...]) * DH**-0.5).astype(BF16)

    lane = lax.broadcasted_iota(jnp.int32, (1, 128), 1)
    left_head = lane < DH

    def attend(place, rec, base, row_count, rows_padded, seg_first, load_queries, store):
        r_id = lax.broadcasted_iota(jnp.int32, (row_count, keys), 0)
        l_id = lax.broadcasted_iota(jnp.int32, (row_count, keys), 1)
        local = jnp.where(r_id < group_rows, r_id >> 6, r_id & 1)
        length = lengths[rec]
        position = start - HALO + base + l_id
        low = local * SEG
        in_window = (
            (l_id >= low)
            & (l_id < low + LEFT + SEG + LOOK)
            & (position >= 0)
            & (position < length)
            & (l_id < WINDOW)
        )
        slot_at = l_id - WINDOW
        slot = slot_at ^ (block * seg_block)
        in_bank = (
            (slot_at >= 0)
            & (slot_at < bank)
            & (slot < seg_first + local)
            & (slot * SEG < length)
        )
        bias_s[place, 0:row_count, :] = jnp.where(in_window | in_bank, 0.0, NEGATIVE_FILL)

        def scores_of(pair):
            cols = pl.ds(pair * 128, 128)
            kcat_s[place, 0:WINDOW, cols] = k_s[rec, pl.ds(pl.multiple_of(base, 16), WINDOW), cols]
            kcat_s[place, WINDOW : WINDOW + bank, cols] = kb_s[rec, :, cols]
            vcat_s[place, pair, 0:WINDOW, 0:128] = v_s[
                rec, pl.ds(pl.multiple_of(base, 16), WINDOW), cols
            ]
            vcat_s[place, pair, WINDOW : WINDOW + bank, 0:128] = vb_s[rec, :, cols]
            query = load_queries(cols)
            zero = jnp.zeros_like(query)
            both = jnp.concatenate(
                [jnp.where(left_head, query, zero), jnp.where(left_head, zero, query)], axis=0
            )
            return dot_nt(both, kcat_s[place, :, cols])

        def probs_of(scores):
            probs = []
            for side in range(2):
                part = scores[side * rows_padded : side * rows_padded + row_count]
                part = part + bias_s[place, 0:row_count, :]
                part = jnp.exp(part - jnp.max(part, axis=1, keepdims=True))
                part = part.astype(BF16)
                if rows_padded > row_count:
                    part = jnp.concatenate(
                        [part, jnp.zeros((rows_padded - row_count, keys), BF16)], axis=0
                    )
                probs.append(part)
            return jnp.concatenate(probs, axis=0)

        def mix(pair, probs):
            mixed = dot(probs, vcat_s[place, pair])
            sides = [
                mixed[side * rows_padded : side * rows_padded + row_count] for side in range(2)
            ]
            value = jnp.where(
                left_head,
                sides[0][:, 0:128] / sides[0][:, 128:256],
                sides[1][:, 0:128] / sides[1][:, 128:256],
            )
            store(pl.ds(pair * 128, 128), value)

        pair_count = width // 128
        scores = scores_of(0)
        for pair in range(pair_count):
            following = scores_of(pair + 1) if pair + 1 < pair_count else None
            mix(pair, probs_of(scores))
            scores = following

    def pair_of_segments(place, rec, pair):
        base = HALO - LEFT + pair * group_rows

        def load_queries(cols):
            return jnp.concatenate(
                [
                    q_s[rec, pl.ds(pl.multiple_of(base + LEFT, 16), group_rows), cols],
                    sq_s[pl.ds(pl.multiple_of((rec * pairs + pair) * 16, 16), 16), cols],
                ],
                axis=0,
            )

        def store(cols, value):
            ctx_s[rec, pl.ds(pl.multiple_of(CONV + pair * group_rows, 16), group_rows), cols] = (
                value[0:group_rows].astype(BF16)
            )
            sctx_s[rec, pl.ds(pl.multiple_of(pair * 8, 8), 8), cols] = value[group_rows:]

        attend(
            place,
            rec,
            base,
            group_rows + 8,
            group_rows + 16,
            start // SEG + 2 * pair,
            load_queries,
            store,
        )

    def segment_before(place, rec):
        def load_queries(cols):
            return q_s[rec, HALO - CONV : HALO, cols]

        def store(cols, value):
            ctx_s[rec, 0:CONV, cols] = value.astype(BF16)

        attend(place, rec, 0, CONV, CONV, start // SEG - 1, load_queries, store)

    ctx_copies = [
        pltpu.make_async_copy(ctx_s.at[rec], ctx_out.at[rec], o_sems.at[rec])
        for rec in range(rec_count)
    ]
    for rec in range(rec_count):
        segment_before(rec % 2, rec)
    for rec in range(rec_count):

        @pl.loop(0, pairs // 2)
        def _(index):
            for place in range(2):
                pair_of_segments(place, rec, 2 * index + place)

        ctx_copies[rec].start()

    for copy in out_copies:
        copy.wait()
    summed = sctx_s[...].reshape(rec_count * pairs * 8, width).astype(BF16)
    vectors = dot(summed[:, 0:half], wa_s[0]) + dot(summed[:, half:width], wa_s[1])
    memory_out[...] = jnp.zeros_like(memory_out)
    segs = 2 * pairs
    for side in range(2):

        @pl.when(core == side)
        def _():
            for rec in range(rec_count):
                rows = [
                    jnp.where(
                        start + seg * SEG < lengths[rec],
                        vectors[rec * pairs * 8 + seg // 2 * 8 + seg % 2 :][0:1],
                        0.0,
                    )
                    for seg in range(segs)
                ]
                memory_out[rec, side * segs : (side + 1) * segs, :] = jnp.concatenate(
                    rows, axis=0
                ).astype(BF16)

    for copy in ctx_copies:
        copy.wait()


def convolution_kernel(
    lengths,
    frames,
    halo,
    ctx,
    wa_o,
    wa_p,
    wc_o,
    wc_p,
    wd_o,
    wd_p,
    wo_o,
    wo_p,
    wi_o,
    wi_p,
    wf_o,
    wf_p,
    gain_conv,
    gain_ffn,
    out,
    x_s,
    ctx_s,
    first_s,
    glu_s,
    g_s,
    act_s,
    fin_s,
    second_s,
    hid_s,
    out_s,
    wa_s,
    wc_s,
    wd_s,
    wo_s,
    wi_s,
    wf_s,
    sems,
    w_sems,
    o_sems,
):
    rec_count, ext, width = x_s.shape
    own = ext - CONV
    half = width // 2
    core = lax.axis_index("mp")
    start = lax.axis_index("tm") * frames.shape[1] + core * own

    loads = [
        load_around(rec, frames, halo, x_s, core, own, CONV, 0, sems.at[rec])
        for rec in range(rec_count)
    ]
    ctx_copies = [
        pltpu.make_async_copy(ctx.at[rec], ctx_s.at[rec], sems.at[rec, 3])
        for rec in range(rec_count)
    ]
    pairs_of = []
    for target, sides in ((wa_s, (wa_o, wa_p)), (wc_s, (wc_o, wc_p)), (wo_s, (wo_o, wo_p))):
        pairs_of += [(sides[0], target.at[0]), (sides[1], target.at[1])]
    for tile in range(width // 128):
        cols = pl.ds(tile * 128 % half, 128)
        pairs_of.append(((wd_o, wd_p)[tile * 128 // half].at[:, cols], wd_s.at[tile]))
    tiles = wi_s.shape[0] // 2
    for target, sides in ((wi_s, (wi_o, wi_p)), (wf_s, (wf_o, wf_p))):
        for side in range(2):
            for tile in range(tiles):
                pairs_of.append(
                    (sides[side].at[:, pl.ds(tile * 256, 256)], target.at[side * tiles + tile])
                )
    copies = [
        pltpu.make_async_copy(source, target, w_sems.at[at])
        for at, (source, target) in enumerate(pairs_of)
    ]
    ctx_copies[0].start()
    for copy in copies[0:2]:
        copy.start()
    loads[0][0]()
    for copy in copies[2:4]:
        copy.start()
    ctx_copies[0].wait()
    loads[0][1]()
    for copy in copies[0:2]:
        copy.wait()
    mid_copies, conv_copies = copies[4:6], copies[6 : 6 + width // 128]
    late_copies = copies[6 + width // 128 :]

    def gated_frames(rec, at, size):
        rows = pl.ds(at if isinstance(at, int) else pl.multiple_of(at, 16), size)
        held = {}

        def project():
            context = ctx_s[rec, rows, :]
            term = dot(context[:, 0:half], wa_s[0]) + dot(context[:, half:width], wa_s[1])
            first = x_s[rec, rows, :].astype(F32) + term
            first_s[rec, rows, :] = first
            position = start - CONV + at + lax.broadcasted_iota(jnp.int32, (size, 1), 0)
            valid = (position >= 0) & (position < lengths[rec])
            normed = norm_rows(first, 0.5 * gain_conv[...])
            held["input"] = jnp.where(valid, normed, 0.0).astype(BF16)

        def gate(part):
            glu = gated(dot(held["input"], wc_s[part, 0]), dot(held["input"], wc_s[part, 1]))
            glu = glu.astype(BF16).astype(F32)
            for tile in range(half // 128):
                glu_s[rec, part * (half // 128) + tile, rows, :] = glu[
                    :, tile * 128 : tile * 128 + 128
                ]

        return [project] + [functools.partial(gate, part) for part in range(2)]

    chunk = g_s.shape[1] - 24
    strip = 64
    conv_tiles = width // 128
    group_taps = 16

    def convolve(rec, at, tile):
        source = glu_s.at[rec, tile, pl.ds(at, chunk + CONV)]
        for shift in range(8):
            size = chunk + (CK - 1 - shift) // 8 * 8
            g_s[shift, pl.ds(0, size), :] = source[pl.ds(CONV - CK + 1 + shift, size), :].astype(
                BF16
            )
        taps = 0.5 * wd_s[tile]
        for top in range(0, chunk, strip):
            total = None
            for first_tap in range(0, CK, group_taps):
                group = None
                for tap in range(first_tap, min(first_tap + group_taps, CK)):
                    rows = pl.ds(top + tap // 8 * 8, strip)
                    product = taps[tap : tap + 1] * g_s[tap % 8, rows, :]
                    group = product if group is None else group + product
                group = group.astype(F32)
                total = group if total is None else total + group
            act_s[tile, pl.ds(at + top, strip), :] = gated(total, total).astype(BF16)

    tiles_all = wi_s.shape[0]
    out_copies = [
        pltpu.make_async_copy(out_s.at[rec], out.at[rec], o_sems.at[rec])
        for rec in range(rec_count)
    ]

    def enter(rec):
        for at in range(0, own, chunk):
            rows = pl.ds(at, chunk)
            sides = [
                jnp.concatenate([act_s[2 * side, rows, :], act_s[2 * side + 1, rows, :]], axis=1)
                for side in range(2)
            ]
            term = dot(sides[0], wo_s[0]) + dot(sides[1], wo_s[1])
            second = first_s[rec, pl.ds(at + CONV, chunk), :] + term
            second_s[rows, :] = second
            fin_s[rows, :] = norm_rows(second, 0.5 * gain_ffn[...]).astype(BF16)

    def up():
        @pl.loop(0, tiles_all // 2)
        def _(index):
            for at in range(2):
                hidden = dot(fin_s[...], wi_s[2 * index + at])
                hid_s[2 * index + at] = gated(hidden, hidden).astype(BF16)

    def down(rec, part):
        cols = pl.ds(part * 256, 256)
        total = second_s[:, cols]
        for tile in range(tiles_all):
            total = total + dot_nt(hid_s[tile], wf_s[tile, cols, :])
        position = start + lax.broadcasted_iota(jnp.int32, (own, 1), 0)
        out_s[rec, :, cols] = jnp.where(position < lengths[rec], total, 0.0).astype(BF16)

    def gate(rec, at):
        for piece in gated_frames(rec, at + CONV, chunk):
            piece()

    before = gated_frames(0, 0, CONV)
    before[0]()
    for copy in copies[2:4]:
        copy.wait()
    for load in ctx_copies[1:]:
        load.start()
    for load in loads[1:]:
        load[0]()
    for copy in copies[4:]:
        copy.start()
    for piece in before[1:]:
        piece()
    for at in range(0, own, chunk):
        gate(0, at)
    for copy in conv_copies:
        copy.wait()
    for rec in range(rec_count):
        if rec == 0:
            for at in range(0, own, chunk):

                @pl.loop(0, 2)
                def _(index):
                    for tile in range(conv_tiles // 2):
                        convolve(rec, at, index * (conv_tiles // 2) + tile)

        if rec + 1 < rec_count:
            ctx_copies[rec + 1].wait()
            loads[rec + 1][1]()
            for piece in gated_frames(rec + 1, 0, CONV):
                piece()
            for at in range(0, own, chunk):
                gate(rec + 1, at)
        if rec == 0:
            for copy in mid_copies:
                copy.wait()
        enter(rec)
        if rec == 0:
            for copy in late_copies:
                copy.wait()
        up()
        for part in range(width // 256):
            down(rec, part)
            if rec + 1 < rec_count:
                each = conv_tiles // (width // 256)
                for at in range(0, own, chunk):
                    for tile in range(each):
                        convolve(rec + 1, at, part * each + tile)
        out_copies[rec].start()
    for copy in out_copies:
        copy.wait()


def vmem(count):
    return [pl.BlockSpec(memory_space=pltpu.VMEM)] * count


def on_device(
    frames,
    lengths,
    memory_in,
    gain_attn,
    w_query,
    w_key,
    w_value,
    w_out,
    gain_conv,
    w_conv_in,
    w_depth,
    w_conv_out,
    gain_ffn,
    w_ffn_in,
    w_ffn_out,
):
    rec_count, frame_count, width = frames.shape
    blocks = lax.axis_size("tm")
    core_count = lax.axis_size("mp")
    core = lax.axis_index("mp")
    own = frame_count // core_count
    seg_block = frame_count // SEG

    def swapped(value):
        return lax.ppermute(value, "mp", [(0, 1), (1, 0)])

    memory = [memory_in]
    for reach in range(1, blocks):
        memory.append(lax.ppermute(memory_in, "tm", [(at, at ^ reach) for at in range(blocks)]))

    ring = [(2 * at, 2 * at + 2) for at in range(blocks - 1)] + [(2 * blocks - 2, 2 * blocks - 1)]
    ring += [(2 * at + 1, 2 * at - 1) for at in range(1, blocks)] + [(1, 0)]
    edge = lax.dynamic_slice_in_dim(frames, (1 - core) * (frame_count - HALO), HALO, 1)
    halo = lax.ppermute(edge, ("tm", "mp"), ring)

    wq, wk, wv = swapped(w_query), swapped(w_key), swapped(w_value)
    wo, wc = swapped(w_out), swapped(w_conv_in)
    wd, wco = swapped(w_depth), swapped(w_conv_out)
    wi, wf = swapped(w_ffn_in), swapped(w_ffn_out)

    ext = HALO + own + LOOK
    bank = seg_block * blocks
    keys = -(-(WINDOW + bank) // 128) * 128
    pairs = own // (2 * SEG)
    group = 2 * SEG + 8
    half = width // 2
    smem = pl.BlockSpec(memory_space=pltpu.SMEM)
    hbm = pl.BlockSpec(memory_space=pltpu.HBM)
    chunk = min(256, own)
    chunks = rec_count * (own // chunk)
    rows = rec_count * own
    hidden_half = w_ffn_in.shape[1]
    ctx, vectors = pl.pallas_call(
        functools.partial(attention_kernel, seg_block=seg_block, blocks=blocks),
        out_shape=(
            jax.ShapeDtypeStruct((rec_count, own + CONV, width), BF16),
            jax.ShapeDtypeStruct((rec_count, 4 * pairs, width), BF16),
        ),
        in_specs=[smem] + [hbm] * (10 + blocks) + vmem(1),
        out_specs=(hbm, vmem(1)[0]),
        scratch_shapes=[
            pltpu.VMEM((rec_count, ext, width), BF16),
            pltpu.VMEM((rec_count, ext, width), BF16),
            pltpu.VMEM((rec_count, ext, width), BF16),
            pltpu.VMEM((rec_count, ext, width), BF16),
            pltpu.VMEM((rec_count, ext, width), BF16),
            pltpu.VMEM((rec_count, bank, width), BF16),
            pltpu.VMEM((rec_count, bank, width), BF16),
            pltpu.VMEM((rec_count, bank, width), BF16),
            pltpu.VMEM((rec_count * pairs * 16, width), BF16),
            pltpu.VMEM((rec_count, own + CONV, width), BF16),
            pltpu.VMEM((rec_count, pairs * 8, width), F32),
            pltpu.VMEM((2, group, keys), F32),
            pltpu.VMEM((2, keys, width), BF16),
            pltpu.VMEM((2, width // 128, keys, 256), BF16),
            pltpu.VMEM((6, width, half), BF16),
            pltpu.VMEM((2, half, width), BF16),
            pltpu.SemaphoreType.DMA((rec_count, 3)),
            pltpu.SemaphoreType.DMA((blocks,)),
            pltpu.SemaphoreType.DMA((8,)),
            pltpu.SemaphoreType.DMA((rec_count,)),
        ],
        compiler_params=pltpu.CompilerParams(vmem_limit_bytes=67043328),
        cost_estimate=pl.CostEstimate(
            flops=10 * 2 * rows * width * half,
            bytes_accessed=8 << 20,
            transcendentals=rows * 2048,
        ),
        name="attend",
    )(
        lengths,
        frames,
        halo,
        *memory,
        w_query,
        wq,
        w_key,
        wk,
        w_value,
        wv,
        w_out,
        wo,
        gain_attn.reshape(1, width),
    )
    others = swapped(vectors)
    output = pl.pallas_call(
        convolution_kernel,
        out_shape=jax.ShapeDtypeStruct((rec_count, own, width), BF16),
        in_specs=[smem] + [hbm] * 15 + vmem(2),
        out_specs=hbm,
        scratch_shapes=[
            pltpu.VMEM((rec_count, own + CONV, width), BF16),
            pltpu.VMEM((rec_count, own + CONV, width), BF16),
            pltpu.VMEM((rec_count, own + CONV, width), F32),
            pltpu.VMEM((rec_count, width // 128, own + CONV, 128), F32),
            pltpu.VMEM((8, chunk + 24, 128), BF16),
            pltpu.VMEM((width // 128, own, 128), BF16),
            pltpu.VMEM((own, width), BF16),
            pltpu.VMEM((own, width), F32),
            pltpu.VMEM((hidden_half // 128, own, 256), BF16),
            pltpu.VMEM((rec_count, own, width), BF16),
            pltpu.VMEM((2, half, width), BF16),
            pltpu.VMEM((2, 2, width, half), BF16),
            pltpu.VMEM((width // 128, CK, 128), BF16),
            pltpu.VMEM((2, half, width), BF16),
            pltpu.VMEM((hidden_half // 128, width, 256), BF16),
            pltpu.VMEM((hidden_half // 128, width, 256), BF16),
            pltpu.SemaphoreType.DMA((rec_count, 4)),
            pltpu.SemaphoreType.DMA((6 + width // 128 + hidden_half // 64,)),
            pltpu.SemaphoreType.DMA((chunks,)),
        ],
        compiler_params=pltpu.CompilerParams(vmem_limit_bytes=65200 << 10),
        cost_estimate=pl.CostEstimate(
            flops=22 * 2 * rows * width * half,
            bytes_accessed=16 << 20,
            transcendentals=rows * 2560,
        ),
        name="rest",
    )(
        lengths,
        frames,
        halo,
        ctx,
        w_out,
        wo,
        w_conv_in,
        wc,
        w_depth,
        wd,
        w_conv_out,
        wco,
        w_ffn_in,
        wi,
        w_ffn_out,
        wf,
        gain_conv.reshape(1, width),
        gain_ffn.reshape(1, width),
    )
    memory_out = vectors + others
    return (output, memory_out)


def solution(mesh):
    placed = (
        P(("groups", "rec"), "tm", None),
        P(("groups", "rec")),
        P(("groups", "rec"), "tm", None),
        P(),
        P(None, "mp"),
        P(None, "mp"),
        P(None, "mp"),
        P("mp", None),
        P(),
        P(None, None, "mp"),
        P(None, "mp"),
        P("mp", None),
        P(),
        P(None, "mp"),
        P(None, "mp"),
    )
    return jax.shard_map(
        on_device,
        mesh=mesh,
        in_specs=placed,
        out_specs=(P(("groups", "rec"), ("tm", "mp"), None), P(("groups", "rec"), "tm", None)),
        check_vma=False,
    )
```

profile of v0, /device:TPU:0, one launch (start us, length us, event | category | flops | bytes accessed | tf_op | source)
XLA Modules:
  0.0 55.0 jit_solution(16343826156763098099)
XLA Ops:
  0.6 0.6 %collective-permute-start.11 = (bf16[512,1024]{1,0:T(8,128)(2,1)}, bf16[512,1024]{1,0:T(8,128)(2,1)}, u32[]{:S(2)}, u32[]{:S(2)}) collective-permute-start(bf16[512,1024]{1,0:T(8,128)(2,1)} %wi_o.1), channel_id=1, source_target_pairs={{0,1},{1,0},{2,3},{3,2},{4,5},{5,4},{6,7},{7,6},{8,9},{9,8},{10,11... | collective-permute-start | bytes 3145736 | tf_op jit(solution)/shard_map/ppermute | solution.py:595
  1.2 0.1 collective-permute-start.12
  1.3 4.0 %collective-permute-start.2 = (bf16[2,16,512]{2,1,0:T(8,128)(2,1)}, bf16[2,16,512]{2,1,0:T(8,128)(2,1)S(1)}, u32[]{:S(2)}, u32[]{:S(2)}) collective-permute-start(bf16[2,16,512]{2,1,0:T(8,128)(2,1)} %refs_3_.1), channel_id=1, source_target_pairs={{0,8},{4,12},{8,0},{12,4},{1,9},{5,13},{9,1},{13,5},{2,10},{6,14},... | collective-permute-start | bytes 98312 | tf_op jit(solution)/shard_map/ppermute | solution.py:599
  5.3 1.6 %collective-permute-start.1 = (bf16[2,16,512]{2,1,0:T(8,128)(2,1)}, bf16[2,16,512]{2,1,0:T(8,128)(2,1)S(1)}, u32[]{:S(2)}, u32[]{:S(2)}) collective-permute-start(bf16[2,16,512]{2,1,0:T(8,128)(2,1)} %refs_3_.1), channel_id=1, source_target_pairs={{0,4},{4,0},{8,12},{12,8},{1,5},{5,1},{9,13},{13,9},{2,6},{6,2},{1... | collective-permute-start | bytes 98312 | tf_op jit(solution)/shard_map/ppermute | solution.py:599
  6.8 0.0 collective-permute-start.3
  6.8 0.5 collective-permute-done.2.refs_5_
  7.4 0.0 collective-permute-start.4
  7.4 2.0 %collective-permute-done.1.refs_4_ = bf16[2,16,512]{2,1,0:T(8,128)(2,1)S(1)} collective-permute-done((bf16[2,16,512]{2,1,0:T(8,128)(2,1)}, bf16[2,16,512]{2,1,0:T(8,128)(2,1)S(1)}, u32[]{:S(2)}, u32[]{:S(2)}) %collective-permute-start.1) | collective-permute-done | bytes 32800 | tf_op jit(solution)/shard_map/ppermute | solution.py:599
  9.4 0.0 collective-permute-start.5
  9.4 1.0 %constant_dynamic-slice_fusion = bf16[2,96,512]{2,1,0:T(8,128)(2,1)S(1)} fusion(bf16[2,1024,512]{2,1,0:T(8,128)(2,1)} %frames.1, s32[]{:T(128)S(6)} %select_n.3), kind=kLoop, calls=%fused_computation | loop fusion | bytes 393220 | tf_op jit(solution)/shard_map/dynamic_slice | solution.py:603
  10.4 2.4 %collective-permute-done.3.refs_6_ = bf16[2,16,512]{2,1,0:T(8,128)(2,1)S(1)} collective-permute-done((bf16[2,16,512]{2,1,0:T(8,128)(2,1)}, bf16[2,16,512]{2,1,0:T(8,128)(2,1)S(1)}, u32[]{:S(2)}, u32[]{:S(2)}) %collective-permute-start.3) | collective-permute-done | bytes 32800 | tf_op jit(solution)/shard_map/ppermute | solution.py:599
  12.8 0.0 collective-permute-start
  12.8 3.2 %collective-permute-done.refs_2_.halo = bf16[2,96,512]{2,1,0:T(8,128)(2,1)S(1)} collective-permute-done((bf16[2,96,512]{2,1,0:T(8,128)(2,1)S(1)}, bf16[2,96,512]{2,1,0:T(8,128)(2,1)S(1)}, u32[]{:S(2)}, u32[]{:S(2)}) %collective-permute-start) | collective-permute-done | bytes 196640 | tf_op jit(solution)/shard_map/ppermute | solution.py:604
  16.0 0.7 %copy-done = bf16[2,96,512]{2,1,0:T(8,128)(2,1)} copy-done((bf16[2,96,512]{2,1,0:T(8,128)(2,1)}, bf16[2,96,512]{2,1,0:T(8,128)(2,1)S(1)}, u32[]{:S(2)}) %copy-start) | copy-done | bytes 196632
  16.6 0.0 collective-permute-start.6
  16.6 0.0 collective-permute-done.4.refs_8_
  16.7 0.6 %collective-permute-start.7 = (bf16[256,512]{1,0:T(8,128)(2,1)}, bf16[256,512]{1,0:T(8,128)(2,1)}, u32[]{:S(2)}, u32[]{:S(2)}) collective-permute-start(bf16[256,512]{1,0:T(8,128)(2,1)} %wa_o.1), channel_id=1, source_target_pairs={{0,1},{1,0},{2,3},{3,2},{4,5},{5,4},{6,7},{7,6},{8,9},{9,8},{10,11... | collective-permute-start | bytes 786440 | tf_op jit(solution)/shard_map/ppermute | solution.py:595
  17.2 0.0 collective-permute-done.5.refs_10_
  17.2 0.1 collective-permute-start.8
  17.3 1.2 %collective-permute-done.6.refs_12_ = bf16[512,256]{1,0:T(8,128)(2,1)} collective-permute-done((bf16[512,256]{1,0:T(8,128)(2,1)}, bf16[512,256]{1,0:T(8,128)(2,1)}, u32[]{:S(2)}, u32[]{:S(2)}) %collective-permute-start.6) | collective-permute-done | bytes 262176 | tf_op jit(solution)/shard_map/ppermute | solution.py:595
  18.5 0.1 collective-permute-start.10
  18.7 0.2 collective-permute-done.7.refs_14_.wa_p
  18.9 12.7 %attend.1 = (bf16[2,544,512]{2,1,0:T(8,128)(2,1)}, bf16[2,16,512]{2,1,0:T(8,128)(2,1)}) custom-call(s32[2]{0:T(128)} %lengths.1, bf16[2,1024,512]{2,1,0:T(8,128)(2,1)} %frames.1, bf16[2,96,512]{2,1,0:T(8,128)(2,1)} %copy-done, bf16[2,16,512]{2,1,0:T(8,128)(2,1)} %refs_3_.1, bf16[2,16,512]{2,1,0:T(8,128)(2,1)} %copy-done.2, bf16[2,16,512]{2,1,0:T(8,128)(2,1)} %copy-done.1, ...), custom_call_target="tpu_custom_call" | custom-call | flops 2684354560 | bytes 8388608 | tf_op jit(solution)/shard_map/attend/pallas_call | solution.py:623
  31.6 0.2 collective-permute-start.13
  31.8 1.2 %collective-permute-done.13 = bf16[2,16,512]{2,1,0:T(8,128)(2,1)S(1)} collective-permute-done((bf16[2,16,512]{2,1,0:T(8,128)(2,1)}, bf16[2,16,512]{2,1,0:T(8,128)(2,1)S(1)}, u32[]{:S(2)}, u32[]{:S(2)}) %collective-permute-start.13) | collective-permute-done | bytes 32800 | tf_op jit(solution)/shard_map/ppermute | solution.py:595
  33.1 0.2 collective-permute-start.9
  33.2 1.4 %add.7 = bf16[2,16,512]{2,1,0:T(8,128)(2,1)} add(bf16[2,16,512]{2,1,0:T(8,128)(2,1)} %get-tuple-element.5, bf16[2,16,512]{2,1,0:T(8,128)(2,1)S(1)} %collective-permute-done.13) | non-fusion elementwise | flops 16384 | bytes 98304 | tf_op jit(solution)/shard_map/add | solution.py:729
  34.6 0.0 collective-permute-done.9.wd_p
  34.6 0.0 collective-permute-done.8.wc_p
  34.6 0.0 collective-permute-done.11.wi_p
  34.7 0.6 %copy-done.4 = bf16[31,256]{1,0:T(8,128)(2,1)} copy-done((bf16[31,256]{1,0:T(8,128)(2,1)}, bf16[31,256]{1,0:T(8,128)(2,1)S(1)}, u32[]{:S(2)}) %copy-start.4) | copy-done | bytes 15896
  35.2 19.7 %rest.1 = bf16[2,512,512]{2,1,0:T(8,128)(2,1)} custom-call(s32[2]{0:T(128)} %lengths.1, bf16[2,1024,512]{2,1,0:T(8,128)(2,1)} %frames.1, bf16[2,96,512]{2,1,0:T(8,128)(2,1)} %copy-done, bf16[2,544,512]{2,1,0:T(8,128)(2,1)} %get-tuple-element.4.ctx, bf16[256,512]{1,0:T(8,128)(2,1)} %wa_o.1, bf16[256,512]{1,0:T(8,128)(2,1)} %collective-permute-done.7.refs_14_.wa_p, ...), custom_call_target="tpu_custom_call" | custom-call | flops 5905580032 | bytes 16777216 | tf_op jit(solution)/shard_map/rest/pallas_call | solution.py:676
  (10 shorter events, 0.0 us)
Async XLA Ops:
  0.6 34.0 %collective-permute-start.11 = (bf16[512,1024]{1,0:T(8,128)(2,1)}, bf16[512,1024]{1,0:T(8,128)(2,1)}, u32[]{:S(2)}, u32[]{:S(2)}) collective-permute-start(bf16[512,1024]{1,0:T(8,128)(2,1)} %wi_o.1), channel_id=1, source_target_pairs={{0,1},{1,0},{2,3},{3,2},{4,5},{5,4},{6,7},{7,6},{8,9},{9,8},{10,11... | collective-permute-start | bytes 3145736 | tf_op jit(solution)/shard_map/ppermute | solution.py:595
  1.2 33.5 %collective-permute-start.12 = (bf16[512,1024]{1,0:T(8,128)(2,1)}, bf16[512,1024]{1,0:T(8,128)(2,1)}, u32[]{:S(2)}, u32[]{:S(2)}) collective-permute-start(bf16[512,1024]{1,0:T(8,128)(2,1)} %wf_o.1), channel_id=1, source_target_pairs={{0,1},{1,0},{2,3},{3,2},{4,5},{5,4},{6,7},{7,6},{8,9},{9,8},{10,11... | collective-permute-start | bytes 3145736 | tf_op jit(solution)/shard_map/ppermute | solution.py:595
  1.3 6.1 %collective-permute-start.2 = (bf16[2,16,512]{2,1,0:T(8,128)(2,1)}, bf16[2,16,512]{2,1,0:T(8,128)(2,1)S(1)}, u32[]{:S(2)}, u32[]{:S(2)}) collective-permute-start(bf16[2,16,512]{2,1,0:T(8,128)(2,1)} %refs_3_.1), channel_id=1, source_target_pairs={{0,8},{4,12},{8,0},{12,4},{1,9},{5,13},{9,1},{13,5},{2,10},{6,14},... | collective-permute-start | bytes 98312 | tf_op jit(solution)/shard_map/ppermute | solution.py:599
  5.3 4.1 %collective-permute-start.1 = (bf16[2,16,512]{2,1,0:T(8,128)(2,1)}, bf16[2,16,512]{2,1,0:T(8,128)(2,1)S(1)}, u32[]{:S(2)}, u32[]{:S(2)}) collective-permute-start(bf16[2,16,512]{2,1,0:T(8,128)(2,1)} %refs_3_.1), channel_id=1, source_target_pairs={{0,4},{4,0},{8,12},{12,8},{1,5},{5,1},{9,13},{13,9},{2,6},{6,2},{1... | collective-permute-start | bytes 98312 | tf_op jit(solution)/shard_map/ppermute | solution.py:599
  6.8 5.9 %collective-permute-start.3 = (bf16[2,16,512]{2,1,0:T(8,128)(2,1)}, bf16[2,16,512]{2,1,0:T(8,128)(2,1)S(1)}, u32[]{:S(2)}, u32[]{:S(2)}) collective-permute-start(bf16[2,16,512]{2,1,0:T(8,128)(2,1)} %refs_3_.1), channel_id=1, source_target_pairs={{0,12},{4,8},{8,4},{12,0},{1,13},{5,9},{9,5},{13,1},{2,14},{6,10},... | collective-permute-start | bytes 98312 | tf_op jit(solution)/shard_map/ppermute | solution.py:599
  7.4 9.3 %copy-start.1 = (bf16[2,16,512]{2,1,0:T(8,128)(2,1)}, bf16[2,16,512]{2,1,0:T(8,128)(2,1)S(1)}, u32[]{:S(2)}) copy-start(bf16[2,16,512]{2,1,0:T(8,128)(2,1)S(1)} %collective-permute-done.2.refs_5_) | copy-start | bytes 98308
  7.4 9.3 %collective-permute-start.4 = (bf16[512,256]{1,0:T(8,128)(2,1)}, bf16[512,256]{1,0:T(8,128)(2,1)}, u32[]{:S(2)}, u32[]{:S(2)}) collective-permute-start(bf16[512,256]{1,0:T(8,128)(2,1)} %refs_7_.1), channel_id=1, source_target_pairs={{0,1},{1,0},{2,3},{3,2},{4,5},{5,4},{6,7},{7,6},{8,9},{9,8},{10,11... | collective-permute-start | bytes 786440 | tf_op jit(solution)/shard_map/ppermute | solution.py:595
  9.4 7.3 %copy-start.2 = (bf16[2,16,512]{2,1,0:T(8,128)(2,1)}, bf16[2,16,512]{2,1,0:T(8,128)(2,1)S(1)}, u32[]{:S(2)}) copy-start(bf16[2,16,512]{2,1,0:T(8,128)(2,1)S(1)} %collective-permute-done.1.refs_4_) | copy-start | bytes 98308
  9.4 7.8 %collective-permute-start.5 = (bf16[512,256]{1,0:T(8,128)(2,1)}, bf16[512,256]{1,0:T(8,128)(2,1)}, u32[]{:S(2)}, u32[]{:S(2)}) collective-permute-start(bf16[512,256]{1,0:T(8,128)(2,1)} %refs_9_.1), channel_id=1, source_target_pairs={{0,1},{1,0},{2,3},{3,2},{4,5},{5,4},{6,7},{7,6},{8,9},{9,8},{10,11... | collective-permute-start | bytes 786440 | tf_op jit(solution)/shard_map/ppermute | solution.py:595
  12.8 4.5 %copy-start.3 = (bf16[2,16,512]{2,1,0:T(8,128)(2,1)}, bf16[2,16,512]{2,1,0:T(8,128)(2,1)S(1)}, u32[]{:S(2)}) copy-start(bf16[2,16,512]{2,1,0:T(8,128)(2,1)S(1)} %collective-permute-done.3.refs_6_) | copy-start | bytes 98308
  12.8 3.2 %collective-permute-start = (bf16[2,96,512]{2,1,0:T(8,128)(2,1)S(1)}, bf16[2,96,512]{2,1,0:T(8,128)(2,1)S(1)}, u32[]{:S(2)}, u32[]{:S(2)}) collective-permute-start(bf16[2,96,512]{2,1,0:T(8,128)(2,1)S(1)} %constant_dynamic-slice_fusion), channel_id=1, source_target_pairs={{0,4},{4,8},{8,12},{12,13},{5,1},{9,5},{13,9},{1,0},{2,6},{6,10},{... | collective-permute-start | bytes 589832 | tf_op jit(solution)/shard_map/ppermute | solution.py:604
  16.0 0.7 %copy-start = (bf16[2,96,512]{2,1,0:T(8,128)(2,1)}, bf16[2,96,512]{2,1,0:T(8,128)(2,1)S(1)}, u32[]{:S(2)}) copy-start(bf16[2,96,512]{2,1,0:T(8,128)(2,1)S(1)} %collective-permute-done.refs_2_.halo) | copy-start | bytes 589828
  16.6 1.9 %collective-permute-start.6 = (bf16[512,256]{1,0:T(8,128)(2,1)}, bf16[512,256]{1,0:T(8,128)(2,1)}, u32[]{:S(2)}, u32[]{:S(2)}) collective-permute-start(bf16[512,256]{1,0:T(8,128)(2,1)} %refs_11_.1), channel_id=1, source_target_pairs={{0,1},{1,0},{2,3},{3,2},{4,5},{5,4},{6,7},{7,6},{8,9},{9,8},{10,11... | collective-permute-start | bytes 786440 | tf_op jit(solution)/shard_map/ppermute | solution.py:595
  16.7 2.2 %collective-permute-start.7 = (bf16[256,512]{1,0:T(8,128)(2,1)}, bf16[256,512]{1,0:T(8,128)(2,1)}, u32[]{:S(2)}, u32[]{:S(2)}) collective-permute-start(bf16[256,512]{1,0:T(8,128)(2,1)} %wa_o.1), channel_id=1, source_target_pairs={{0,1},{1,0},{2,3},{3,2},{4,5},{5,4},{6,7},{7,6},{8,9},{9,8},{10,11... | collective-permute-start | bytes 786440 | tf_op jit(solution)/shard_map/ppermute | solution.py:595
  17.2 17.4 %collective-permute-start.8 = (bf16[2,512,256]{2,1,0:T(8,128)(2,1)}, bf16[2,512,256]{2,1,0:T(8,128)(2,1)}, u32[]{:S(2)}, u32[]{:S(2)}) collective-permute-start(bf16[2,512,256]{2,1,0:T(8,128)(2,1)} %wc_o.1), channel_id=1, source_target_pairs={{0,1},{1,0},{2,3},{3,2},{4,5},{5,4},{6,7},{7,6},{8,9},{9,8},{10,11... | collective-permute-start | bytes 1572872 | tf_op jit(solution)/shard_map/ppermute | solution.py:595
  18.5 16.1 %collective-permute-start.10 = (bf16[256,512]{1,0:T(8,128)(2,1)}, bf16[256,512]{1,0:T(8,128)(2,1)}, u32[]{:S(2)}, u32[]{:S(2)}) collective-permute-start(bf16[256,512]{1,0:T(8,128)(2,1)} %wo_o.1), channel_id=1, source_target_pairs={{0,1},{1,0},{2,3},{3,2},{4,5},{5,4},{6,7},{7,6},{8,9},{9,8},{10,11... | collective-permute-start | bytes 786440 | tf_op jit(solution)/shard_map/ppermute | solution.py:595
  31.6 1.5 %collective-permute-start.13 = (bf16[2,16,512]{2,1,0:T(8,128)(2,1)}, bf16[2,16,512]{2,1,0:T(8,128)(2,1)S(1)}, u32[]{:S(2)}, u32[]{:S(2)}) collective-permute-start(bf16[2,16,512]{2,1,0:T(8,128)(2,1)} %get-tuple-element.5), channel_id=1, source_target_pairs={{0,1},{1,0},{2,3},{3,2},{4,5},{5,4},{6,7},{7,6},{8,9},{9,8},{10,11... | collective-permute-start | bytes 98312 | tf_op jit(solution)/shard_map/ppermute | solution.py:595
  33.1 1.6 %collective-permute-start.9 = (bf16[31,256]{1,0:T(8,128)(2,1)}, bf16[31,256]{1,0:T(8,128)(2,1)S(1)}, u32[]{:S(2)}, u32[]{:S(2)}) collective-permute-start(bf16[31,256]{1,0:T(8,128)(2,1)} %wd_o.1), channel_id=1, source_target_pairs={{0,1},{1,0},{2,3},{3,2},{4,5},{5,4},{6,7},{7,6},{8,9},{9,8},{10,11... | collective-permute-start | bytes 47624 | tf_op jit(solution)/shard_map/ppermute | solution.py:595
  34.6 0.6 %copy-start.4 = (bf16[31,256]{1,0:T(8,128)(2,1)}, bf16[31,256]{1,0:T(8,128)(2,1)S(1)}, u32[]{:S(2)}) copy-start(bf16[31,256]{1,0:T(8,128)(2,1)S(1)} %collective-permute-done.9.wd_p) | copy-start | bytes 47620
where the time goes:
time: 55.3 us; the launch traced here: 55 us
  Pallas kernels  32.3 us (58%)
  waiting for transfers between devices  10.8 us (20%)
  starting transfers between devices  7.46 us (13%)
  local copies, waits for them, and re-layouts  2.19 us (4%)
  other arithmetic  1.38 us (2%)
  between operations  0.86 us (2%)
    pallas_call x1, Pallas kernels, on_device(): pl.pallas_call(convolution_kernel, out_shape=jax.ShapeDtypeStruct((rec_co...  19.7 us
    pallas_call x1, Pallas kernels, on_device(): pl.pallas_call(functools.partial(attention_kernel, seg_block=seg_block, b...  12.7 us
    ppermute x3, starting transfers between devices, on_device(): lax.ppermute(memory_in, 'tm', [(at, at ^ reach) for at in range(blocks)])  5.58 us
    ppermute x3, waiting for transfers between devices, on_device(): lax.ppermute(memory_in, 'tm', [(at, at ^ reach) for at in range(blocks)])  4.95 us
    ppermute x1, waiting for transfers between devices, on_device(): halo = lax.ppermute(edge, ('tm', 'mp'), ring)  3.19 us
    ppermute x10, waiting for transfers between devices, swapped(): return lax.ppermute(value, 'mp', [(0, 1), (1, 0)])  2.68 us
    ppermute x10, starting transfers between devices, swapped(): return lax.ppermute(value, 'mp', [(0, 1), (1, 0)])  1.87 us
    add x1, other arithmetic, on_device(): memory_out = vectors + others  1.38 us
  transfers between devices with their start and end apart: 14, of which 7 were waited for; matrix products, arithmetic and copies ran while one was open for 4% of the time, Pallas kernels for 23%

commit v1 on v0

--- a/solution.py
+++ b/solution.py
@@ -82,6 +82,10 @@
                     copy.wait()
 
     return start, wait
+
+
+def copy_kernel(source, target):
+    target[...] = source[...]
 
 
 def attention_kernel(*refs, seg_block, blocks):
@@ -153,20 +157,32 @@
     wq_o, wq_p, wk_o, wk_p, wv_o, wv_p = [w_s.at[at] for at in range(6)]
     chunks = 3
     step = ext // chunks
+
+    def normalise(rec, part):
+        rows = pl.ds(part * step, step)
+        normed = norm_rows(x_s[rec, rows, :].astype(F32), gain_attn[...]).astype(BF16)
+        n_s[rec, rows, :] = normed
+        return normed
+
+    def project(rec, part, normed):
+        rows = pl.ds(part * step, step)
+        for side, (wq, wk, wv) in enumerate(((wq_o, wk_o, wv_o), (wq_p, wk_p, wv_p))):
+            cols = pl.ds(side * half, half)
+            q_s[rec, rows, cols] = (dot(normed, wq[...]) * DH**-0.5).astype(BF16)
+            k_s[rec, rows, cols] = dot(normed, wk[...]).astype(BF16)
+            v_s[rec, rows, cols] = dot(normed, wv[...]).astype(BF16)
+
+    loads[0][1]()
+    for part in range(chunks):
+        normalise(0, part)
+    for load in loads[1:]:
+        load[1]()
+    for copy in weight_copies:
+        copy.wait()
     for rec in range(rec_count):
-        loads[rec][1]()
-        if rec == 0:
-            for copy in weight_copies:
-                copy.wait()
         for part in range(chunks):
-            rows = pl.ds(part * step, step)
-            normed = norm_rows(x_s[rec, rows, :].astype(F32), gain_attn[...]).astype(BF16)
-            n_s[rec, rows, :] = normed
-            for side, (wq, wk, wv) in enumerate(((wq_o, wk_o, wv_o), (wq_p, wk_p, wv_p))):
-                cols = pl.ds(side * half, half)
-                q_s[rec, rows, cols] = (dot(normed, wq[...]) * DH**-0.5).astype(BF16)
-                k_s[rec, rows, cols] = dot(normed, wk[...]).astype(BF16)
-                v_s[rec, rows, cols] = dot(normed, wv[...]).astype(BF16)
+            normed = n_s[rec, part * step : (part + 1) * step, :] if rec == 0 else normalise(rec, part)
+            project(rec, part, normed)
 
     mean_rows = pairs * 16
     row_id = lax.broadcasted_iota(jnp.int32, (mean_rows, own), 0)
@@ -450,11 +466,13 @@
         return [project] + [functools.partial(gate, part) for part in range(2)]
 
     chunk = g_s.shape[1] - 24
+    chunks = own // chunk
     strip = 64
     conv_tiles = width // 128
     group_taps = 16
 
     def convolve(rec, at, tile):
+        at = at if isinstance(at, int) else pl.multiple_of(at, chunk)
         source = glu_s.at[rec, tile, pl.ds(at, chunk + CONV)]
         for shift in range(8):
             size = chunk + (CK - 1 - shift) // 8 * 8
@@ -493,11 +511,11 @@
             fin_s[rows, :] = norm_rows(second, 0.5 * gain_ffn[...]).astype(BF16)
 
     def up():
-        @pl.loop(0, tiles_all // 2)
+        @pl.loop(0, tiles_all // 4)
         def _(index):
-            for at in range(2):
-                hidden = dot(fin_s[...], wi_s[2 * index + at])
-                hid_s[2 * index + at] = gated(hidden, hidden).astype(BF16)
+            for at in range(4):
+                hidden = dot(fin_s[...], wi_s[4 * index + at])
+                hid_s[4 * index + at] = gated(hidden, hidden).astype(BF16)
 
     def down(rec, part):
         cols = pl.ds(part * 256, 256)
@@ -506,6 +524,22 @@
             total = total + dot_nt(hid_s[tile], wf_s[tile, cols, :])
         position = start + lax.broadcasted_iota(jnp.int32, (own, 1), 0)
         out_s[rec, :, cols] = jnp.where(position < lengths[rec], total, 0.0).astype(BF16)
+
+    def down_beside(rec, conv_rec):
+        units = chunks * conv_tiles // 2
+        size = own // units
+
+        @pl.loop(0, units)
+        def _(index):
+            rows = pl.ds(pl.multiple_of(index * size, size), size)
+            total = second_s[rows, :]
+            for tile in range(tiles_all):
+                total = total + dot_nt(hid_s[tile, rows, :], wf_s[tile])
+            position = start + index * size + lax.broadcasted_iota(jnp.int32, (size, 1), 0)
+            out_s[rec, rows, :] = jnp.where(position < lengths[rec], total, 0.0).astype(BF16)
+            for at in range(2):
+                unit = 2 * index + at
+                convolve(conv_rec, unit // conv_tiles * chunk, unit % conv_tiles)
 
     def gate(rec, at):
         for piece in gated_frames(rec, at + CONV, chunk):
@@ -551,13 +585,11 @@
             for copy in late_copies:
                 copy.wait()
         up()
-        for part in range(width // 256):
-            down(rec, part)
-            if rec + 1 < rec_count:
-                each = conv_tiles // (width // 256)
-                for at in range(0, own, chunk):
-                    for tile in range(each):
-                        convolve(rec + 1, at, part * each + tile)
+        if rec + 1 < rec_count:
+            down_beside(rec, rec + 1)
+        else:
+            for part in range(width // 256):
+                down(rec, part)
         out_copies[rec].start()
     for copy in out_copies:
         copy.wait()
@@ -620,6 +652,14 @@
     chunks = rec_count * (own // chunk)
     rows = rec_count * own
     hidden_half = w_ffn_in.shape[1]
+    gain_first = pl.pallas_call(
+        copy_kernel,
+        out_shape=jax.ShapeDtypeStruct((1, width), F32),
+        in_specs=vmem(1),
+        out_specs=vmem(1)[0],
+        compiler_params=pltpu.CompilerParams(vmem_limit_bytes=67043328),
+        name="hold",
+    )(gain_attn.reshape(1, width))
     ctx, vectors = pl.pallas_call(
         functools.partial(attention_kernel, seg_block=seg_block, blocks=blocks),
         out_shape=(
@@ -657,21 +697,7 @@
             transcendentals=rows * 2048,
         ),
         name="attend",
-    )(
-        lengths,
-        frames,
-        halo,
-        *memory,
-        w_query,
-        wq,
-        w_key,
-        wk,
-        w_value,
-        wv,
-        w_out,
-        wo,
-        gain_attn.reshape(1, width),
-    )
+    )(lengths, frames, halo, *memory, w_query, wq, w_key, wk, w_value, wv, w_out, wo, gain_first)
     others = swapped(vectors)
     output = pl.pallas_call(
         convolution_kernel,

time: 55.3 us -> 54.2 us (0.980)
  waiting for transfers between devices: 10.8 us -> 9.48 us
    ppermute x10, waiting for transfers between devices: 2.68 us -> 1.34 us  [swapped(): return lax.ppermute(value, 'mp', [(0, 1), (1, 0)])]
    pallas_call x0 -> x1, Pallas kernels: none -> 1.27 us  [on_device(): pl.pallas_call(copy_kernel, out_shape=jax.ShapeDtypeStruct((1, width), F3...]
    pallas_call x1, Pallas kernels: 19.7 us -> 18.8 us  [on_device(): pl.pallas_call(convolution_kernel, out_shape=jax.ShapeDtypeStruct((rec_co...]
  transfers between devices with their start and end apart: 14 -> 14, of which waited for: 7 -> 5; matrix products, arithmetic and copies ran while one was open for 4% -> 4% of each run, Pallas kernels for 23% -> 25%
where the time goes in v1:
time: 54.2 us; the launch traced here: 53.8 us
  Pallas kernels  32.3 us (60%)
  waiting for transfers between devices  9.48 us (17%)
  starting transfers between devices  7.64 us (14%)
  local copies, waits for them, and re-layouts  2.19 us (4%)
  other arithmetic  1.38 us (3%)
  between operations  0.86 us (2%)
    pallas_call x1, Pallas kernels, on_device(): pl.pallas_call(convolution_kernel, out_shape=jax.ShapeDtypeStruct((rec_co...  18.8 us
    pallas_call x1, Pallas kernels, on_device(): pl.pallas_call(functools.partial(attention_kernel, seg_block=seg_block, b...  12.2 us
    ppermute x3, starting transfers between devices, on_device(): lax.ppermute(memory_in, 'tm', [(at, at ^ reach) for at in range(blocks)])  5.58 us
    ppermute x3, waiting for transfers between devices, on_device(): lax.ppermute(memory_in, 'tm', [(at, at ^ reach) for at in range(blocks)])  4.95 us
    ppermute x1, waiting for transfers between devices, on_device(): halo = lax.ppermute(edge, ('tm', 'mp'), ring)  3.19 us
    ppermute x10, starting transfers between devices, swapped(): return lax.ppermute(value, 'mp', [(0, 1), (1, 0)])  2.06 us
    add x1, other arithmetic, on_device(): memory_out = vectors + others  1.38 us
    ppermute x10, waiting for transfers between devices, swapped(): return lax.ppermute(value, 'mp', [(0, 1), (1, 0)])  1.34 us
  transfers between devices with their start and end apart: 14, of which 5 were waited for; matrix products, arithmetic and copies ran while one was open for 4% of the time, Pallas kernels for 25%

profile of v1, /device:TPU:0, one launch (start us, length us, event | category | flops | bytes accessed | tf_op | source)
XLA Modules:
  0.0 53.8 jit_solution(11109705411207019553)
XLA Ops:
  0.6 0.6 %collective-permute-start.11 = (bf16[512,1024]{1,0:T(8,128)(2,1)}, bf16[512,1024]{1,0:T(8,128)(2,1)}, u32[]{:S(2)}, u32[]{:S(2)}) collective-permute-start(bf16[512,1024]{1,0:T(8,128)(2,1)} %wi_o.1), channel_id=1, source_target_pairs={{0,1},{1,0},{2,3},{3,2},{4,5},{5,4},{6,7},{7,6},{8,9},{9,8},{10,11... | collective-permute-start | bytes 3145736 | tf_op jit(solution)/shard_map/ppermute | solution.py:627
  1.2 0.1 collective-permute-start.12
  1.3 4.0 %collective-permute-start.2 = (bf16[2,16,512]{2,1,0:T(8,128)(2,1)}, bf16[2,16,512]{2,1,0:T(8,128)(2,1)S(1)}, u32[]{:S(2)}, u32[]{:S(2)}) collective-permute-start(bf16[2,16,512]{2,1,0:T(8,128)(2,1)} %refs_3_.1), channel_id=1, source_target_pairs={{0,8},{4,12},{8,0},{12,4},{1,9},{5,13},{9,1},{13,5},{2,10},{6,14},... | collective-permute-start | bytes 98312 | tf_op jit(solution)/shard_map/ppermute | solution.py:631
  5.3 1.6 %collective-permute-start.1 = (bf16[2,16,512]{2,1,0:T(8,128)(2,1)}, bf16[2,16,512]{2,1,0:T(8,128)(2,1)S(1)}, u32[]{:S(2)}, u32[]{:S(2)}) collective-permute-start(bf16[2,16,512]{2,1,0:T(8,128)(2,1)} %refs_3_.1), channel_id=1, source_target_pairs={{0,4},{4,0},{8,12},{12,8},{1,5},{5,1},{9,13},{13,9},{2,6},{6,2},{1... | collective-permute-start | bytes 98312 | tf_op jit(solution)/shard_map/ppermute | solution.py:631
  6.8 0.0 collective-permute-start.3
  6.8 0.5 collective-permute-done.2.refs_5_
  7.4 0.0 collective-permute-start.4
  7.4 2.0 %collective-permute-done.1.refs_4_ = bf16[2,16,512]{2,1,0:T(8,128)(2,1)S(1)} collective-permute-done((bf16[2,16,512]{2,1,0:T(8,128)(2,1)}, bf16[2,16,512]{2,1,0:T(8,128)(2,1)S(1)}, u32[]{:S(2)}, u32[]{:S(2)}) %collective-permute-start.1) | collective-permute-done | bytes 32800 | tf_op jit(solution)/shard_map/ppermute | solution.py:631
  9.4 0.0 collective-permute-start.5
  9.4 1.0 %constant_dynamic-slice_fusion = bf16[2,96,512]{2,1,0:T(8,128)(2,1)S(1)} fusion(bf16[2,1024,512]{2,1,0:T(8,128)(2,1)} %frames.1, s32[]{:T(128)S(6)} %select_n.3), kind=kLoop, calls=%fused_computation | loop fusion | bytes 393220 | tf_op jit(solution)/shard_map/dynamic_slice | solution.py:635
  10.4 2.4 %collective-permute-done.3.refs_6_ = bf16[2,16,512]{2,1,0:T(8,128)(2,1)S(1)} collective-permute-done((bf16[2,16,512]{2,1,0:T(8,128)(2,1)}, bf16[2,16,512]{2,1,0:T(8,128)(2,1)S(1)}, u32[]{:S(2)}, u32[]{:S(2)}) %collective-permute-start.3) | collective-permute-done | bytes 32800 | tf_op jit(solution)/shard_map/ppermute | solution.py:631
  12.8 0.0 collective-permute-start
  12.8 3.2 %collective-permute-done.refs_2_.halo = bf16[2,96,512]{2,1,0:T(8,128)(2,1)S(1)} collective-permute-done((bf16[2,96,512]{2,1,0:T(8,128)(2,1)S(1)}, bf16[2,96,512]{2,1,0:T(8,128)(2,1)S(1)}, u32[]{:S(2)}, u32[]{:S(2)}) %collective-permute-start) | collective-permute-done | bytes 196640 | tf_op jit(solution)/shard_map/ppermute | solution.py:636
  16.0 0.7 %copy-done = bf16[2,96,512]{2,1,0:T(8,128)(2,1)} copy-done((bf16[2,96,512]{2,1,0:T(8,128)(2,1)}, bf16[2,96,512]{2,1,0:T(8,128)(2,1)S(1)}, u32[]{:S(2)}) %copy-start) | copy-done | bytes 196632
  16.6 0.0 collective-permute-start.6
  16.6 0.0 collective-permute-done.4.refs_8_
  16.7 0.6 %collective-permute-start.7 = (bf16[256,512]{1,0:T(8,128)(2,1)}, bf16[256,512]{1,0:T(8,128)(2,1)}, u32[]{:S(2)}, u32[]{:S(2)}) collective-permute-start(bf16[256,512]{1,0:T(8,128)(2,1)} %wa_o.1), channel_id=1, source_target_pairs={{0,1},{1,0},{2,3},{3,2},{4,5},{5,4},{6,7},{7,6},{8,9},{9,8},{10,11... | collective-permute-start | bytes 786440 | tf_op jit(solution)/shard_map/ppermute | solution.py:627
  17.2 0.0 collective-permute-done.5.refs_10_
  17.2 0.1 collective-permute-start.8
  17.3 1.3 %hold.1.refs_15_ = f32[1,512]{1,0:T(1,128)} custom-call(f32[1,512]{1,0:T(1,128)} %bitcast.3), custom_call_target="tpu_custom_call" | custom-call | tf_op jit(solution)/shard_map/hold/pallas_call | solution.py:655
  18.6 0.4 collective-permute-start.10
  19.0 12.2 %attend.1 = (bf16[2,544,512]{2,1,0:T(8,128)(2,1)}, bf16[2,16,512]{2,1,0:T(8,128)(2,1)}) custom-call(s32[2]{0:T(128)} %lengths.1, bf16[2,1024,512]{2,1,0:T(8,128)(2,1)} %frames.1, bf16[2,96,512]{2,1,0:T(8,128)(2,1)} %copy-done, bf16[2,16,512]{2,1,0:T(8,128)(2,1)} %refs_3_.1, bf16[2,16,512]{2,1,0:T(8,128)(2,1)} %copy-done.2, bf16[2,16,512]{2,1,0:T(8,128)(2,1)} %copy-done.1, ...), custom_call_target="tpu_custom_call" | custom-call | flops 2684354560 | bytes 8388608 | tf_op jit(solution)/shard_map/attend/pallas_call | solution.py:663
  31.2 0.2 collective-permute-start.13
  31.4 1.3 %collective-permute-done.13 = bf16[2,16,512]{2,1,0:T(8,128)(2,1)S(1)} collective-permute-done((bf16[2,16,512]{2,1,0:T(8,128)(2,1)}, bf16[2,16,512]{2,1,0:T(8,128)(2,1)S(1)}, u32[]{:S(2)}, u32[]{:S(2)}) %collective-permute-start.13) | collective-permute-done | bytes 32800 | tf_op jit(solution)/shard_map/ppermute | solution.py:627
  32.7 0.2 collective-permute-start.9
  32.8 1.4 %add.7 = bf16[2,16,512]{2,1,0:T(8,128)(2,1)} add(bf16[2,16,512]{2,1,0:T(8,128)(2,1)} %get-tuple-element.5, bf16[2,16,512]{2,1,0:T(8,128)(2,1)S(1)} %collective-permute-done.13) | non-fusion elementwise | flops 16384 | bytes 98304 | tf_op jit(solution)/shard_map/add | solution.py:755
  34.2 0.0 collective-permute-done.9.wd_p
  34.2 0.0 collective-permute-done.10.wo_p
  34.2 0.0 collective-permute-done.11.wi_p
  34.3 0.0 collective-permute-done.12.wf_p
  34.3 0.6 %copy-done.4 = bf16[31,256]{1,0:T(8,128)(2,1)} copy-done((bf16[31,256]{1,0:T(8,128)(2,1)}, bf16[31,256]{1,0:T(8,128)(2,1)S(1)}, u32[]{:S(2)}) %copy-start.4) | copy-done | bytes 15896
  34.8 18.8 %rest.1 = bf16[2,512,512]{2,1,0:T(8,128)(2,1)} custom-call(s32[2]{0:T(128)} %lengths.1, bf16[2,1024,512]{2,1,0:T(8,128)(2,1)} %frames.1, bf16[2,96,512]{2,1,0:T(8,128)(2,1)} %copy-done, bf16[2,544,512]{2,1,0:T(8,128)(2,1)} %get-tuple-element.4.ctx, bf16[256,512]{1,0:T(8,128)(2,1)} %wa_o.1, bf16[256,512]{1,0:T(8,128)(2,1)} %collective-permute-done.7.refs_14_.wa_p, ...), custom_call_target="tpu_custom_call" | custom-call | flops 5905580032 | bytes 16777216 | tf_op jit(solution)/shard_map/rest/pallas_call | solution.py:702
  (11 shorter events, 0.0 us)
Async XLA Ops:
  0.6 33.6 %collective-permute-start.11 = (bf16[512,1024]{1,0:T(8,128)(2,1)}, bf16[512,1024]{1,0:T(8,128)(2,1)}, u32[]{:S(2)}, u32[]{:S(2)}) collective-permute-start(bf16[512,1024]{1,0:T(8,128)(2,1)} %wi_o.1), channel_id=1, source_target_pairs={{0,1},{1,0},{2,3},{3,2},{4,5},{5,4},{6,7},{7,6},{8,9},{9,8},{10,11... | collective-permute-start | bytes 3145736 | tf_op jit(solution)/shard_map/ppermute | solution.py:627
  1.2 33.1 %collective-permute-start.12 = (bf16[512,1024]{1,0:T(8,128)(2,1)}, bf16[512,1024]{1,0:T(8,128)(2,1)}, u32[]{:S(2)}, u32[]{:S(2)}) collective-permute-start(bf16[512,1024]{1,0:T(8,128)(2,1)} %wf_o.1), channel_id=1, source_target_pairs={{0,1},{1,0},{2,3},{3,2},{4,5},{5,4},{6,7},{7,6},{8,9},{9,8},{10,11... | collective-permute-start | bytes 3145736 | tf_op jit(solution)/shard_map/ppermute | solution.py:627
  1.3 6.1 %collective-permute-start.2 = (bf16[2,16,512]{2,1,0:T(8,128)(2,1)}, bf16[2,16,512]{2,1,0:T(8,128)(2,1)S(1)}, u32[]{:S(2)}, u32[]{:S(2)}) collective-permute-start(bf16[2,16,512]{2,1,0:T(8,128)(2,1)} %refs_3_.1), channel_id=1, source_target_pairs={{0,8},{4,12},{8,0},{12,4},{1,9},{5,13},{9,1},{13,5},{2,10},{6,14},... | collective-permute-start | bytes 98312 | tf_op jit(solution)/shard_map/ppermute | solution.py:631
  5.3 4.1 %collective-permute-start.1 = (bf16[2,16,512]{2,1,0:T(8,128)(2,1)}, bf16[2,16,512]{2,1,0:T(8,128)(2,1)S(1)}, u32[]{:S(2)}, u32[]{:S(2)}) collective-permute-start(bf16[2,16,512]{2,1,0:T(8,128)(2,1)} %refs_3_.1), channel_id=1, source_target_pairs={{0,4},{4,0},{8,12},{12,8},{1,5},{5,1},{9,13},{13,9},{2,6},{6,2},{1... | collective-permute-start | bytes 98312 | tf_op jit(solution)/shard_map/ppermute | solution.py:631
  6.8 5.9 %collective-permute-start.3 = (bf16[2,16,512]{2,1,0:T(8,128)(2,1)}, bf16[2,16,512]{2,1,0:T(8,128)(2,1)S(1)}, u32[]{:S(2)}, u32[]{:S(2)}) collective-permute-start(bf16[2,16,512]{2,1,0:T(8,128)(2,1)} %refs_3_.1), channel_id=1, source_target_pairs={{0,12},{4,8},{8,4},{12,0},{1,13},{5,9},{9,5},{13,1},{2,14},{6,10},... | collective-permute-start | bytes 98312 | tf_op jit(solution)/shard_map/ppermute | solution.py:631
  7.4 9.3 %copy-start.1 = (bf16[2,16,512]{2,1,0:T(8,128)(2,1)}, bf16[2,16,512]{2,1,0:T(8,128)(2,1)S(1)}, u32[]{:S(2)}) copy-start(bf16[2,16,512]{2,1,0:T(8,128)(2,1)S(1)} %collective-permute-done.2.refs_5_) | copy-start | bytes 98308
  7.4 9.3 %collective-permute-start.4 = (bf16[512,256]{1,0:T(8,128)(2,1)}, bf16[512,256]{1,0:T(8,128)(2,1)}, u32[]{:S(2)}, u32[]{:S(2)}) collective-permute-start(bf16[512,256]{1,0:T(8,128)(2,1)} %refs_7_.1), channel_id=1, source_target_pairs={{0,1},{1,0},{2,3},{3,2},{4,5},{5,4},{6,7},{7,6},{8,9},{9,8},{10,11... | collective-permute-start | bytes 786440 | tf_op jit(solution)/shard_map/ppermute | solution.py:627
  9.4 7.3 %copy-start.2 = (bf16[2,16,512]{2,1,0:T(8,128)(2,1)}, bf16[2,16,512]{2,1,0:T(8,128)(2,1)S(1)}, u32[]{:S(2)}) copy-start(bf16[2,16,512]{2,1,0:T(8,128)(2,1)S(1)} %collective-permute-done.1.refs_4_) | copy-start | bytes 98308
  9.4 7.8 %collective-permute-start.5 = (bf16[512,256]{1,0:T(8,128)(2,1)}, bf16[512,256]{1,0:T(8,128)(2,1)}, u32[]{:S(2)}, u32[]{:S(2)}) collective-permute-start(bf16[512,256]{1,0:T(8,128)(2,1)} %refs_9_.1), channel_id=1, source_target_pairs={{0,1},{1,0},{2,3},{3,2},{4,5},{5,4},{6,7},{7,6},{8,9},{9,8},{10,11... | collective-permute-start | bytes 786440 | tf_op jit(solution)/shard_map/ppermute | solution.py:627
  12.8 4.5 %copy-start.3 = (bf16[2,16,512]{2,1,0:T(8,128)(2,1)}, bf16[2,16,512]{2,1,0:T(8,128)(2,1)S(1)}, u32[]{:S(2)}) copy-start(bf16[2,16,512]{2,1,0:T(8,128)(2,1)S(1)} %collective-permute-done.3.refs_6_) | copy-start | bytes 98308
  12.8 3.2 %collective-permute-start = (bf16[2,96,512]{2,1,0:T(8,128)(2,1)S(1)}, bf16[2,96,512]{2,1,0:T(8,128)(2,1)S(1)}, u32[]{:S(2)}, u32[]{:S(2)}) collective-permute-start(bf16[2,96,512]{2,1,0:T(8,128)(2,1)S(1)} %constant_dynamic-slice_fusion), channel_id=1, source_target_pairs={{0,4},{4,8},{8,12},{12,13},{5,1},{9,5},{13,9},{1,0},{2,6},{6,10},{... | collective-permute-start | bytes 589832 | tf_op jit(solution)/shard_map/ppermute | solution.py:636
  16.0 0.7 %copy-start = (bf16[2,96,512]{2,1,0:T(8,128)(2,1)}, bf16[2,96,512]{2,1,0:T(8,128)(2,1)S(1)}, u32[]{:S(2)}) copy-start(bf16[2,96,512]{2,1,0:T(8,128)(2,1)S(1)} %collective-permute-done.refs_2_.halo) | copy-start | bytes 589828
  16.6 2.0 %collective-permute-start.6 = (bf16[512,256]{1,0:T(8,128)(2,1)}, bf16[512,256]{1,0:T(8,128)(2,1)}, u32[]{:S(2)}, u32[]{:S(2)}) collective-permute-start(bf16[512,256]{1,0:T(8,128)(2,1)} %refs_11_.1), channel_id=1, source_target_pairs={{0,1},{1,0},{2,3},{3,2},{4,5},{5,4},{6,7},{7,6},{8,9},{9,8},{10,11... | collective-permute-start | bytes 786440 | tf_op jit(solution)/shard_map/ppermute | solution.py:627
  16.7 2.4 %collective-permute-start.7 = (bf16[256,512]{1,0:T(8,128)(2,1)}, bf16[256,512]{1,0:T(8,128)(2,1)}, u32[]{:S(2)}, u32[]{:S(2)}) collective-permute-start(bf16[256,512]{1,0:T(8,128)(2,1)} %wa_o.1), channel_id=1, source_target_pairs={{0,1},{1,0},{2,3},{3,2},{4,5},{5,4},{6,7},{7,6},{8,9},{9,8},{10,11... | collective-permute-start | bytes 786440 | tf_op jit(solution)/shard_map/ppermute | solution.py:627
  17.2 17.0 %collective-permute-start.8 = (bf16[2,512,256]{2,1,0:T(8,128)(2,1)}, bf16[2,512,256]{2,1,0:T(8,128)(2,1)}, u32[]{:S(2)}, u32[]{:S(2)}) collective-permute-start(bf16[2,512,256]{2,1,0:T(8,128)(2,1)} %wc_o.1), channel_id=1, source_target_pairs={{0,1},{1,0},{2,3},{3,2},{4,5},{5,4},{6,7},{7,6},{8,9},{9,8},{10,11... | collective-permute-start | bytes 1572872 | tf_op jit(solution)/shard_map/ppermute | solution.py:627
  18.6 15.6 %collective-permute-start.10 = (bf16[256,512]{1,0:T(8,128)(2,1)}, bf16[256,512]{1,0:T(8,128)(2,1)}, u32[]{:S(2)}, u32[]{:S(2)}) collective-permute-start(bf16[256,512]{1,0:T(8,128)(2,1)} %wo_o.1), channel_id=1, source_target_pairs={{0,1},{1,0},{2,3},{3,2},{4,5},{5,4},{6,7},{7,6},{8,9},{9,8},{10,11... | collective-permute-start | bytes 786440 | tf_op jit(solution)/shard_map/ppermute | solution.py:627
  31.2 1.5 %collective-permute-start.13 = (bf16[2,16,512]{2,1,0:T(8,128)(2,1)}, bf16[2,16,512]{2,1,0:T(8,128)(2,1)S(1)}, u32[]{:S(2)}, u32[]{:S(2)}) collective-permute-start(bf16[2,16,512]{2,1,0:T(8,128)(2,1)} %get-tuple-element.5), channel_id=1, source_target_pairs={{0,1},{1,0},{2,3},{3,2},{4,5},{5,4},{6,7},{7,6},{8,9},{9,8},{10,11... | collective-permute-start | bytes 98312 | tf_op jit(solution)/shard_map/ppermute | solution.py:627
  32.7 1.5 %collective-permute-start.9 = (bf16[31,256]{1,0:T(8,128)(2,1)}, bf16[31,256]{1,0:T(8,128)(2,1)S(1)}, u32[]{:S(2)}, u32[]{:S(2)}) collective-permute-start(bf16[31,256]{1,0:T(8,128)(2,1)} %wd_o.1), channel_id=1, source_target_pairs={{0,1},{1,0},{2,3},{3,2},{4,5},{5,4},{6,7},{7,6},{8,9},{9,8},{10,11... | collective-permute-start | bytes 47624 | tf_op jit(solution)/shard_map/ppermute | solution.py:627
  34.2 0.6 %copy-start.4 = (bf16[31,256]{1,0:T(8,128)(2,1)}, bf16[31,256]{1,0:T(8,128)(2,1)S(1)}, u32[]{:S(2)}) copy-start(bf16[31,256]{1,0:T(8,128)(2,1)S(1)} %collective-permute-done.9.wd_p) | copy-start | bytes 47620

commit v2 on v1

--- a/solution.py
+++ b/solution.py
@@ -467,7 +467,7 @@
 
     chunk = g_s.shape[1] - 24
     chunks = own // chunk
-    strip = 64
+    strip = 32
     conv_tiles = width // 128
     group_taps = 16
 
@@ -497,6 +497,14 @@
         pltpu.make_async_copy(out_s.at[rec], out.at[rec], o_sems.at[rec])
         for rec in range(rec_count)
     ]
+    out_halves = [
+        pltpu.make_async_copy(
+            out_s.at[rec_count - 1, :, pl.ds(part * 256, 256)],
+            out.at[rec_count - 1, :, pl.ds(part * 256, 256)],
+            o_sems.at[rec_count - 1 + part],
+        )
+        for part in range(width // 256)
+    ]
 
     def enter(rec):
         for at in range(0, own, chunk):
@@ -582,16 +590,21 @@
                 copy.wait()
         enter(rec)
         if rec == 0:
-            for copy in late_copies:
+            for copy in late_copies[: len(late_copies) // 2]:
                 copy.wait()
         up()
+        if rec == 0:
+            for copy in late_copies[len(late_copies) // 2 :]:
+                copy.wait()
         if rec + 1 < rec_count:
             down_beside(rec, rec + 1)
         else:
             for part in range(width // 256):
                 down(rec, part)
-        out_copies[rec].start()
-    for copy in out_copies:
+                out_halves[part].start()
+        if rec + 1 < rec_count:
+            out_copies[rec].start()
+    for copy in out_copies[:-1] + out_halves:
         copy.wait()
 
 

time: 54.2 us -> 54.1 us (level)
  no operation moved by 1% of the time
where the time goes in v2:
time: 54.1 us; the launch traced here: 53.8 us
  Pallas kernels  32.2 us (60%)
  waiting for transfers between devices  9.48 us (18%)
  starting transfers between devices  7.64 us (14%)
  local copies, waits for them, and re-layouts  2.19 us (4%)
  other arithmetic  1.38 us (3%)
  between operations  0.86 us (2%)
    pallas_call x1, Pallas kernels, on_device(): pl.pallas_call(convolution_kernel, out_shape=jax.ShapeDtypeStruct((rec_co...  18.8 us
    pallas_call x1, Pallas kernels, on_device(): pl.pallas_call(functools.partial(attention_kernel, seg_block=seg_block, b...  12.2 us
    ppermute x3, starting transfers between devices, on_device(): lax.ppermute(memory_in, 'tm', [(at, at ^ reach) for at in range(blocks)])  5.58 us
    ppermute x3, waiting for transfers between devices, on_device(): lax.ppermute(memory_in, 'tm', [(at, at ^ reach) for at in range(blocks)])  4.95 us
    ppermute x1, waiting for transfers between devices, on_device(): halo = lax.ppermute(edge, ('tm', 'mp'), ring)  3.19 us
    ppermute x10, starting transfers between devices, swapped(): return lax.ppermute(value, 'mp', [(0, 1), (1, 0)])  2.06 us
    add x1, other arithmetic, on_device(): memory_out = vectors + others  1.38 us
    ppermute x10, waiting for transfers between devices, swapped(): return lax.ppermute(value, 'mp', [(0, 1), (1, 0)])  1.34 us
  transfers between devices with their start and end apart: 14, of which 5 were waited for; matrix products, arithmetic and copies ran while one was open for 4% of the time, Pallas kernels for 25%

profile of v2, /device:TPU:0, one launch (start us, length us, event | category | flops | bytes accessed | tf_op | source)
XLA Modules:
  0.0 53.8 jit_solution(7529509213112559584)
XLA Ops:
  0.6 0.6 %collective-permute-start.11 = (bf16[512,1024]{1,0:T(8,128)(2,1)}, bf16[512,1024]{1,0:T(8,128)(2,1)}, u32[]{:S(2)}, u32[]{:S(2)}) collective-permute-start(bf16[512,1024]{1,0:T(8,128)(2,1)} %wi_o.1), channel_id=1, source_target_pairs={{0,1},{1,0},{2,3},{3,2},{4,5},{5,4},{6,7},{7,6},{8,9},{9,8},{10,11... | collective-permute-start | bytes 3145736 | tf_op jit(solution)/shard_map/ppermute | solution.py:640
  1.2 0.1 collective-permute-start.12
  1.3 4.0 %collective-permute-start.2 = (bf16[2,16,512]{2,1,0:T(8,128)(2,1)}, bf16[2,16,512]{2,1,0:T(8,128)(2,1)S(1)}, u32[]{:S(2)}, u32[]{:S(2)}) collective-permute-start(bf16[2,16,512]{2,1,0:T(8,128)(2,1)} %refs_3_.1), channel_id=1, source_target_pairs={{0,8},{4,12},{8,0},{12,4},{1,9},{5,13},{9,1},{13,5},{2,10},{6,14},... | collective-permute-start | bytes 98312 | tf_op jit(solution)/shard_map/ppermute | solution.py:644
  5.3 1.6 %collective-permute-start.1 = (bf16[2,16,512]{2,1,0:T(8,128)(2,1)}, bf16[2,16,512]{2,1,0:T(8,128)(2,1)S(1)}, u32[]{:S(2)}, u32[]{:S(2)}) collective-permute-start(bf16[2,16,512]{2,1,0:T(8,128)(2,1)} %refs_3_.1), channel_id=1, source_target_pairs={{0,4},{4,0},{8,12},{12,8},{1,5},{5,1},{9,13},{13,9},{2,6},{6,2},{1... | collective-permute-start | bytes 98312 | tf_op jit(solution)/shard_map/ppermute | solution.py:644
  6.8 0.0 collective-permute-start.3
  6.8 0.5 collective-permute-done.2.refs_5_
  7.4 0.0 collective-permute-start.4
  7.4 2.0 %collective-permute-done.1.refs_4_ = bf16[2,16,512]{2,1,0:T(8,128)(2,1)S(1)} collective-permute-done((bf16[2,16,512]{2,1,0:T(8,128)(2,1)}, bf16[2,16,512]{2,1,0:T(8,128)(2,1)S(1)}, u32[]{:S(2)}, u32[]{:S(2)}) %collective-permute-start.1) | collective-permute-done | bytes 32800 | tf_op jit(solution)/shard_map/ppermute | solution.py:644
  9.4 0.0 collective-permute-start.5
  9.4 1.0 %constant_dynamic-slice_fusion = bf16[2,96,512]{2,1,0:T(8,128)(2,1)S(1)} fusion(bf16[2,1024,512]{2,1,0:T(8,128)(2,1)} %frames.1, s32[]{:T(128)S(6)} %select_n.3), kind=kLoop, calls=%fused_computation | loop fusion | bytes 393220 | tf_op jit(solution)/shard_map/dynamic_slice | solution.py:648
  10.4 2.4 %collective-permute-done.3.refs_6_ = bf16[2,16,512]{2,1,0:T(8,128)(2,1)S(1)} collective-permute-done((bf16[2,16,512]{2,1,0:T(8,128)(2,1)}, bf16[2,16,512]{2,1,0:T(8,128)(2,1)S(1)}, u32[]{:S(2)}, u32[]{:S(2)}) %collective-permute-start.3) | collective-permute-done | bytes 32800 | tf_op jit(solution)/shard_map/ppermute | solution.py:644
  12.8 0.0 collective-permute-start
  12.8 3.2 %collective-permute-done.refs_2_.halo = bf16[2,96,512]{2,1,0:T(8,128)(2,1)S(1)} collective-permute-done((bf16[2,96,512]{2,1,0:T(8,128)(2,1)S(1)}, bf16[2,96,512]{2,1,0:T(8,128)(2,1)S(1)}, u32[]{:S(2)}, u32[]{:S(2)}) %collective-permute-start) | collective-permute-done | bytes 196640 | tf_op jit(solution)/shard_map/ppermute | solution.py:649
  16.0 0.7 %copy-done = bf16[2,96,512]{2,1,0:T(8,128)(2,1)} copy-done((bf16[2,96,512]{2,1,0:T(8,128)(2,1)}, bf16[2,96,512]{2,1,0:T(8,128)(2,1)S(1)}, u32[]{:S(2)}) %copy-start) | copy-done | bytes 196632
  16.6 0.0 collective-permute-start.6
  16.6 0.0 collective-permute-done.4.refs_8_
  16.7 0.6 %collective-permute-start.7 = (bf16[256,512]{1,0:T(8,128)(2,1)}, bf16[256,512]{1,0:T(8,128)(2,1)}, u32[]{:S(2)}, u32[]{:S(2)}) collective-permute-start(bf16[256,512]{1,0:T(8,128)(2,1)} %wa_o.1), channel_id=1, source_target_pairs={{0,1},{1,0},{2,3},{3,2},{4,5},{5,4},{6,7},{7,6},{8,9},{9,8},{10,11... | collective-permute-start | bytes 786440 | tf_op jit(solution)/shard_map/ppermute | solution.py:640
  17.2 0.0 collective-permute-done.5.refs_10_
  17.2 0.1 collective-permute-start.8
  17.3 1.3 %hold.1.refs_15_ = f32[1,512]{1,0:T(1,128)} custom-call(f32[1,512]{1,0:T(1,128)} %bitcast.3), custom_call_target="tpu_custom_call" | custom-call | tf_op jit(solution)/shard_map/hold/pallas_call | solution.py:668
  18.6 0.4 collective-permute-start.10
  19.0 12.2 %attend.1 = (bf16[2,544,512]{2,1,0:T(8,128)(2,1)}, bf16[2,16,512]{2,1,0:T(8,128)(2,1)}) custom-call(s32[2]{0:T(128)} %lengths.1, bf16[2,1024,512]{2,1,0:T(8,128)(2,1)} %frames.1, bf16[2,96,512]{2,1,0:T(8,128)(2,1)} %copy-done, bf16[2,16,512]{2,1,0:T(8,128)(2,1)} %refs_3_.1, bf16[2,16,512]{2,1,0:T(8,128)(2,1)} %copy-done.2, bf16[2,16,512]{2,1,0:T(8,128)(2,1)} %copy-done.1, ...), custom_call_target="tpu_custom_call" | custom-call | flops 2684354560 | bytes 8388608 | tf_op jit(solution)/shard_map/attend/pallas_call | solution.py:676
  31.2 0.2 collective-permute-start.13
  31.4 1.3 %collective-permute-done.13 = bf16[2,16,512]{2,1,0:T(8,128)(2,1)S(1)} collective-permute-done((bf16[2,16,512]{2,1,0:T(8,128)(2,1)}, bf16[2,16,512]{2,1,0:T(8,128)(2,1)S(1)}, u32[]{:S(2)}, u32[]{:S(2)}) %collective-permute-start.13) | collective-permute-done | bytes 32800 | tf_op jit(solution)/shard_map/ppermute | solution.py:640
  32.7 0.2 collective-permute-start.9
  32.8 1.4 %add.7 = bf16[2,16,512]{2,1,0:T(8,128)(2,1)} add(bf16[2,16,512]{2,1,0:T(8,128)(2,1)} %get-tuple-element.5, bf16[2,16,512]{2,1,0:T(8,128)(2,1)S(1)} %collective-permute-done.13) | non-fusion elementwise | flops 16384 | bytes 98304 | tf_op jit(solution)/shard_map/add | solution.py:768
  34.2 0.0 collective-permute-done.9.wd_p
  34.2 0.0 collective-permute-done.10.wo_p
  34.2 0.0 collective-permute-done.11.wi_p
  34.3 0.0 collective-permute-done.12.wf_p
  34.3 0.6 %copy-done.4 = bf16[31,256]{1,0:T(8,128)(2,1)} copy-done((bf16[31,256]{1,0:T(8,128)(2,1)}, bf16[31,256]{1,0:T(8,128)(2,1)S(1)}, u32[]{:S(2)}) %copy-start.4) | copy-done | bytes 15896
  34.8 18.8 %rest.1 = bf16[2,512,512]{2,1,0:T(8,128)(2,1)} custom-call(s32[2]{0:T(128)} %lengths.1, bf16[2,1024,512]{2,1,0:T(8,128)(2,1)} %frames.1, bf16[2,96,512]{2,1,0:T(8,128)(2,1)} %copy-done, bf16[2,544,512]{2,1,0:T(8,128)(2,1)} %get-tuple-element.4.ctx, bf16[256,512]{1,0:T(8,128)(2,1)} %wa_o.1, bf16[256,512]{1,0:T(8,128)(2,1)} %collective-permute-done.7.refs_14_.wa_p, ...), custom_call_target="tpu_custom_call" | custom-call | flops 5905580032 | bytes 16777216 | tf_op jit(solution)/shard_map/rest/pallas_call | solution.py:715
  (11 shorter events, 0.0 us)
Async XLA Ops:
  0.6 33.6 %collective-permute-start.11 = (bf16[512,1024]{1,0:T(8,128)(2,1)}, bf16[512,1024]{1,0:T(8,128)(2,1)}, u32[]{:S(2)}, u32[]{:S(2)}) collective-permute-start(bf16[512,1024]{1,0:T(8,128)(2,1)} %wi_o.1), channel_id=1, source_target_pairs={{0,1},{1,0},{2,3},{3,2},{4,5},{5,4},{6,7},{7,6},{8,9},{9,8},{10,11... | collective-permute-start | bytes 3145736 | tf_op jit(solution)/shard_map/ppermute | solution.py:640
  1.2 33.1 %collective-permute-start.12 = (bf16[512,1024]{1,0:T(8,128)(2,1)}, bf16[512,1024]{1,0:T(8,128)(2,1)}, u32[]{:S(2)}, u32[]{:S(2)}) collective-permute-start(bf16[512,1024]{1,0:T(8,128)(2,1)} %wf_o.1), channel_id=1, source_target_pairs={{0,1},{1,0},{2,3},{3,2},{4,5},{5,4},{6,7},{7,6},{8,9},{9,8},{10,11... | collective-permute-start | bytes 3145736 | tf_op jit(solution)/shard_map/ppermute | solution.py:640
  1.3 6.1 %collective-permute-start.2 = (bf16[2,16,512]{2,1,0:T(8,128)(2,1)}, bf16[2,16,512]{2,1,0:T(8,128)(2,1)S(1)}, u32[]{:S(2)}, u32[]{:S(2)}) collective-permute-start(bf16[2,16,512]{2,1,0:T(8,128)(2,1)} %refs_3_.1), channel_id=1, source_target_pairs={{0,8},{4,12},{8,0},{12,4},{1,9},{5,13},{9,1},{13,5},{2,10},{6,14},... | collective-permute-start | bytes 98312 | tf_op jit(solution)/shard_map/ppermute | solution.py:644
  5.3 4.1 %collective-permute-start.1 = (bf16[2,16,512]{2,1,0:T(8,128)(2,1)}, bf16[2,16,512]{2,1,0:T(8,128)(2,1)S(1)}, u32[]{:S(2)}, u32[]{:S(2)}) collective-permute-start(bf16[2,16,512]{2,1,0:T(8,128)(2,1)} %refs_3_.1), channel_id=1, source_target_pairs={{0,4},{4,0},{8,12},{12,8},{1,5},{5,1},{9,13},{13,9},{2,6},{6,2},{1... | collective-permute-start | bytes 98312 | tf_op jit(solution)/shard_map/ppermute | solution.py:644
  6.8 5.9 %collective-permute-start.3 = (bf16[2,16,512]{2,1,0:T(8,128)(2,1)}, bf16[2,16,512]{2,1,0:T(8,128)(2,1)S(1)}, u32[]{:S(2)}, u32[]{:S(2)}) collective-permute-start(bf16[2,16,512]{2,1,0:T(8,128)(2,1)} %refs_3_.1), channel_id=1, source_target_pairs={{0,12},{4,8},{8,4},{12,0},{1,13},{5,9},{9,5},{13,1},{2,14},{6,10},... | collective-permute-start | bytes 98312 | tf_op jit(solution)/shard_map/ppermute | solution.py:644
  7.4 9.3 %copy-start.1 = (bf16[2,16,512]{2,1,0:T(8,128)(2,1)}, bf16[2,16,512]{2,1,0:T(8,128)(2,1)S(1)}, u32[]{:S(2)}) copy-start(bf16[2,16,512]{2,1,0:T(8,128)(2,1)S(1)} %collective-permute-done.2.refs_5_) | copy-start | bytes 98308
  7.4 9.3 %collective-permute-start.4 = (bf16[512,256]{1,0:T(8,128)(2,1)}, bf16[512,256]{1,0:T(8,128)(2,1)}, u32[]{:S(2)}, u32[]{:S(2)}) collective-permute-start(bf16[512,256]{1,0:T(8,128)(2,1)} %refs_7_.1), channel_id=1, source_target_pairs={{0,1},{1,0},{2,3},{3,2},{4,5},{5,4},{6,7},{7,6},{8,9},{9,8},{10,11... | collective-permute-start | bytes 786440 | tf_op jit(solution)/shard_map/ppermute | solution.py:640
  9.4 7.3 %copy-start.2 = (bf16[2,16,512]{2,1,0:T(8,128)(2,1)}, bf16[2,16,512]{2,1,0:T(8,128)(2,1)S(1)}, u32[]{:S(2)}) copy-start(bf16[2,16,512]{2,1,0:T(8,128)(2,1)S(1)} %collective-permute-done.1.refs_4_) | copy-start | bytes 98308
  9.4 7.8 %collective-permute-start.5 = (bf16[512,256]{1,0:T(8,128)(2,1)}, bf16[512,256]{1,0:T(8,128)(2,1)}, u32[]{:S(2)}, u32[]{:S(2)}) collective-permute-start(bf16[512,256]{1,0:T(8,128)(2,1)} %refs_9_.1), channel_id=1, source_target_pairs={{0,1},{1,0},{2,3},{3,2},{4,5},{5,4},{6,7},{7,6},{8,9},{9,8},{10,11... | collective-permute-start | bytes 786440 | tf_op jit(solution)/shard_map/ppermute | solution.py:640
  12.8 4.5 %copy-start.3 = (bf16[2,16,512]{2,1,0:T(8,128)(2,1)}, bf16[2,16,512]{2,1,0:T(8,128)(2,1)S(1)}, u32[]{:S(2)}) copy-start(bf16[2,16,512]{2,1,0:T(8,128)(2,1)S(1)} %collective-permute-done.3.refs_6_) | copy-start | bytes 98308
  12.8 3.2 %collective-permute-start = (bf16[2,96,512]{2,1,0:T(8,128)(2,1)S(1)}, bf16[2,96,512]{2,1,0:T(8,128)(2,1)S(1)}, u32[]{:S(2)}, u32[]{:S(2)}) collective-permute-start(bf16[2,96,512]{2,1,0:T(8,128)(2,1)S(1)} %constant_dynamic-slice_fusion), channel_id=1, source_target_pairs={{0,4},{4,8},{8,12},{12,13},{5,1},{9,5},{13,9},{1,0},{2,6},{6,10},{... | collective-permute-start | bytes 589832 | tf_op jit(solution)/shard_map/ppermute | solution.py:649
  16.0 0.7 %copy-start = (bf16[2,96,512]{2,1,0:T(8,128)(2,1)}, bf16[2,96,512]{2,1,0:T(8,128)(2,1)S(1)}, u32[]{:S(2)}) copy-start(bf16[2,96,512]{2,1,0:T(8,128)(2,1)S(1)} %collective-permute-done.refs_2_.halo) | copy-start | bytes 589828
  16.6 2.0 %collective-permute-start.6 = (bf16[512,256]{1,0:T(8,128)(2,1)}, bf16[512,256]{1,0:T(8,128)(2,1)}, u32[]{:S(2)}, u32[]{:S(2)}) collective-permute-start(bf16[512,256]{1,0:T(8,128)(2,1)} %refs_11_.1), channel_id=1, source_target_pairs={{0,1},{1,0},{2,3},{3,2},{4,5},{5,4},{6,7},{7,6},{8,9},{9,8},{10,11... | collective-permute-start | bytes 786440 | tf_op jit(solution)/shard_map/ppermute | solution.py:640
  16.7 2.4 %collective-permute-start.7 = (bf16[256,512]{1,0:T(8,128)(2,1)}, bf16[256,512]{1,0:T(8,128)(2,1)}, u32[]{:S(2)}, u32[]{:S(2)}) collective-permute-start(bf16[256,512]{1,0:T(8,128)(2,1)} %wa_o.1), channel_id=1, source_target_pairs={{0,1},{1,0},{2,3},{3,2},{4,5},{5,4},{6,7},{7,6},{8,9},{9,8},{10,11... | collective-permute-start | bytes 786440 | tf_op jit(solution)/shard_map/ppermute | solution.py:640
  17.2 17.0 %collective-permute-start.8 = (bf16[2,512,256]{2,1,0:T(8,128)(2,1)}, bf16[2,512,256]{2,1,0:T(8,128)(2,1)}, u32[]{:S(2)}, u32[]{:S(2)}) collective-permute-start(bf16[2,512,256]{2,1,0:T(8,128)(2,1)} %wc_o.1), channel_id=1, source_target_pairs={{0,1},{1,0},{2,3},{3,2},{4,5},{5,4},{6,7},{7,6},{8,9},{9,8},{10,11... | collective-permute-start | bytes 1572872 | tf_op jit(solution)/shard_map/ppermute | solution.py:640
  18.6 15.6 %collective-permute-start.10 = (bf16[256,512]{1,0:T(8,128)(2,1)}, bf16[256,512]{1,0:T(8,128)(2,1)}, u32[]{:S(2)}, u32[]{:S(2)}) collective-permute-start(bf16[256,512]{1,0:T(8,128)(2,1)} %wo_o.1), channel_id=1, source_target_pairs={{0,1},{1,0},{2,3},{3,2},{4,5},{5,4},{6,7},{7,6},{8,9},{9,8},{10,11... | collective-permute-start | bytes 786440 | tf_op jit(solution)/shard_map/ppermute | solution.py:640
  31.2 1.5 %collective-permute-start.13 = (bf16[2,16,512]{2,1,0:T(8,128)(2,1)}, bf16[2,16,512]{2,1,0:T(8,128)(2,1)S(1)}, u32[]{:S(2)}, u32[]{:S(2)}) collective-permute-start(bf16[2,16,512]{2,1,0:T(8,128)(2,1)} %get-tuple-element.5), channel_id=1, source_target_pairs={{0,1},{1,0},{2,3},{3,2},{4,5},{5,4},{6,7},{7,6},{8,9},{9,8},{10,11... | collective-permute-start | bytes 98312 | tf_op jit(solution)/shard_map/ppermute | solution.py:640
  32.7 1.5 %collective-permute-start.9 = (bf16[31,256]{1,0:T(8,128)(2,1)}, bf16[31,256]{1,0:T(8,128)(2,1)S(1)}, u32[]{:S(2)}, u32[]{:S(2)}) collective-permute-start(bf16[31,256]{1,0:T(8,128)(2,1)} %wd_o.1), channel_id=1, source_target_pairs={{0,1},{1,0},{2,3},{3,2},{4,5},{5,4},{6,7},{7,6},{8,9},{9,8},{10,11... | collective-permute-start | bytes 47624 | tf_op jit(solution)/shard_map/ppermute | solution.py:640
  34.2 0.6 %copy-start.4 = (bf16[31,256]{1,0:T(8,128)(2,1)}, bf16[31,256]{1,0:T(8,128)(2,1)S(1)}, u32[]{:S(2)}) copy-start(bf16[31,256]{1,0:T(8,128)(2,1)S(1)} %collective-permute-done.9.wd_p) | copy-start | bytes 47620
